TPU v7x, 32 devices: a whole 2x2x4 slice. The times are simulated.
32 devices in a mesh: grp: 2 (over x), head: 4 (over z), seq: 4 (over y, core).
Axes of the slice: x: 2, y: 2, z: 4, core: 2. Of those that a mesh axis runs over, the one named last changes fastest.
Arguments:
- queries: bfloat16 [64, 512, 128], P('head', 'seq'), may hold values from -6 to 6
- keys: bfloat16 [4, 512, 128], P('head', 'seq'), may hold values from -6 to 6
- values: bfloat16 [4, 512, 128], P('head', 'seq'), may hold values from -6 to 6
- feature_map: bfloat16 [64, 128, 128], P('head'), may hold values from -0.5 to 0.5
Outputs:
- feature_grad: float32 [64, 128, 128], P('head', ('grp', 'seq'))
All inputs are finite; a program needn't handle non-finite values.
Results may differ from a plain program's by a relative error of at most 0.0044.
Values may be sent and summed in bfloat16 or wider, within the bound.
No kernel may reach another device: no remote copies, remote signals or barrier semaphores. Data moves between devices by JAX's collectives and lax.ppermute only.
A program may use at most 128 MiB of HBM per device.

v0:
```python
import jax
import jax.numpy as jnp
from jax import lax
from jax.sharding import PartitionSpec as P


def prefix(part, axis, combine, identity, reverse):
    count = lax.axis_size(axis)
    place = lax.axis_index(axis)
    ahead = count - 1 - place if reverse else place
    gathered = jax.tree.map(lambda a: lax.all_gather(a, axis), part)
    state = jax.tree.map(lambda a, e: jnp.zeros_like(a) + jnp.asarray(e, a.dtype), part, identity)

    def one(hop, state):
        source = count - 1 - hop if reverse else hop
        return combine(
            state, jax.tree.map(lambda a: lax.dynamic_index_in_dim(a, source, 0, False), gathered)
        )

    return lax.fori_loop(0, ahead, one, state)


def shifted(value, axis, steps):
    count = lax.axis_size(axis)
    first, last = (max(0, -steps), min(count, count - steps))
    return lax.ppermute(value, axis, [(source, source + steps) for source in range(first, last)])


def add_pair(earlier, later):
    return (earlier[0] + later[0], earlier[1] + later[1])


def attend_step(query_rows, own_start):
    scale = 1.0 / jnp.sqrt(jnp.float32(query_rows.shape[-1]))

    def step(carry, pieces, start):
        key_piece, value_piece = pieces
        scores = (
            jnp.einsum("hid,jd->hij", query_rows, key_piece[0], preferred_element_type=jnp.float32)
            * scale
        )
        shape_two = (query_rows.shape[1], key_piece.shape[1])
        row_pos = own_start + lax.broadcasted_iota(jnp.int32, shape_two, 0)
        col_pos = lax.broadcasted_iota(jnp.int32, shape_two, 1)
        weights = jnp.where((col_pos <= row_pos)[None], jnp.exp(scores), jnp.float32(0.0))
        denom = jnp.sum(weights, axis=2)
        numer = jnp.einsum(
            "hij,jd->hid",
            weights.astype(jnp.bfloat16),
            value_piece[0],
            preferred_element_type=jnp.float32,
        )
        return (numer, denom)

    return step


def empty_carry(query_rows):
    return (jnp.zeros(query_rows.shape, jnp.float32), jnp.zeros(query_rows.shape[:2], jnp.float32))


def finish(carry):
    return (carry[0] / carry[1][:, :, None]).astype(jnp.bfloat16)


def student_part(queries, keys, values, feature_map, target, total_tokens, active):
    highest = lax.Precision.HIGHEST
    query_rows = queries.astype(jnp.float32)
    key_rows = keys[0].astype(jnp.float32)
    value_rows = values[0].astype(jnp.float32)
    weights_f = feature_map.astype(jnp.float32)
    tokens_here = key_rows.shape[0]
    lower = jnp.tril(jnp.ones((tokens_here, tokens_here), jnp.float32))
    heads_here = weights_f.shape[0]
    feats = weights_f.shape[2]
    width = value_rows.shape[1]
    zeros_pair = (
        jnp.zeros((heads_here, feats, width), jnp.float32),
        jnp.zeros((heads_here, feats), jnp.float32),
    )

    def key_features(wmat):
        return jnp.exp(jnp.einsum("td,hdf->htf", key_rows, wmat, precision=highest))

    def local_states(wmat):
        phi_k = key_features(wmat)
        return (
            jnp.einsum("htf,td->hfd", phi_k, value_rows, precision=highest),
            jnp.sum(phi_k, axis=1),
        )

    def outputs(wmat, prior, prior_sum):
        phi_q = jnp.exp(jnp.einsum("htd,hdf->htf", query_rows, wmat, precision=highest))
        phi_k = key_features(wmat)
        scores = jnp.einsum("hif,hjf->hij", phi_q, phi_k, precision=highest) * lower[None]
        numer = jnp.einsum("hij,jd->hid", scores, value_rows, precision=highest)
        numer = numer + jnp.einsum("hif,hfd->hid", phi_q, prior, precision=highest)
        denom = jnp.sum(scores, axis=2) + jnp.einsum(
            "hif,hf->hi", phi_q, prior_sum, precision=highest
        )
        return numer / denom[:, :, None]

    states = lax.cond(active, lambda: local_states(weights_f), lambda: zeros_pair)
    prior, prior_sum = prefix(states, "seq", add_pair, zeros_pair, False)

    def backward_outputs():
        student, out_back = jax.vjp(outputs, weights_f, prior, prior_sum)
        cotangent = 2.0 * (student - target.astype(jnp.float32)) / jnp.float32(total_tokens)
        return out_back(cotangent)

    def backward_none():
        return (jnp.zeros_like(weights_f), zeros_pair[0], zeros_pair[1])

    grad_direct, grad_prior, grad_prior_sum = lax.cond(active, backward_outputs, backward_none)
    later = prefix((grad_prior, grad_prior_sum), "seq", add_pair, zeros_pair, True)

    def backward_states():
        state_back = jax.vjp(local_states, weights_f)[1]
        return grad_direct + state_back(later)[0]

    return lax.cond(active, backward_states, lambda: jnp.zeros_like(weights_f))


def per_device(queries, keys, values, feature_map):
    grp_index = lax.axis_index("grp")
    tokens_here = keys.shape[1]
    own_start = lax.axis_index("seq") * tokens_here
    total_tokens = tokens_here * lax.axis_size("seq")
    is_teacher = grp_index == 0
    inner = attend_step(queries, own_start)
    guarded_carry = empty_carry(queries)
    pieces = (
        lax.all_gather(keys, "seq", axis=1, tiled=True),
        lax.all_gather(values, "seq", axis=1, tiled=True),
    )
    start = jnp.int32(0)
    carry = lax.cond(is_teacher, lambda: inner(guarded_carry, pieces, start), lambda: guarded_carry)
    teacher_local = lax.cond(
        is_teacher, lambda: finish(carry), lambda: jnp.zeros(queries.shape, jnp.bfloat16)
    )
    target = shifted(teacher_local, "grp", 1)
    grad_term = student_part(
        queries, keys, values, feature_map, target, total_tokens, grp_index == 1
    )
    return lax.psum_scatter(grad_term, ("grp", "seq"), scatter_dimension=1, tiled=True)


def solution(mesh):
    return jax.shard_map(
        per_device,
        mesh=mesh,
        in_specs=(
            P("head", "seq", None),
            P("head", "seq", None),
            P("head", "seq", None),
            P("head", None, None),
        ),
        out_specs=P("head", ("grp", "seq"), None),
        check_vma=False,
    )
```

profile of v0, /device:TPU:0, one launch (start us, length us, event | category | flops | bytes accessed | tf_op | source)
XLA Modules:
  0.0 174.9 jit_solution(9679085192851748379)
XLA Ops:
  6.5 1.1 convert_element_type.40
  7.7 0.8 bitcast_convert_fusion
  8.5 0.8 bitcast_convert_fusion.1
  9.4 1.0 copy-done.2
  10.4 6.5 %all_gather.34 = bf16[1,512,128]{2,1,0:T(8,128)(2,1)S(1)} all-gather(bf16[1,128,128]{2,1,0:T(8,128)(2,1)S(1)} %copy-done.3), channel_id=1, replica_groups=mesh['grp'=2,'head'=4,'seq'=4] {'seq'}, dimensions={1}, use_global_device_ids=true | all-gather | bytes 163840 | tf_op jit(solution)/shard_map/all_gather | solution.py:133
  17.0 5.6 %all_gather.35 = bf16[1,512,128]{2,1,0:T(8,128)(2,1)S(1)} all-gather(bf16[1,128,128]{2,1,0:T(8,128)(2,1)S(1)} %copy-done.4), channel_id=1, replica_groups=mesh['grp'=2,'head'=4,'seq'=4] {'seq'}, dimensions={1}, use_global_device_ids=true | all-gather | bytes 163840 | tf_op jit(solution)/shard_map/all_gather | solution.py:134
  22.6 3.1 %conditional.6 = (f32[16,128,128]{2,1,0:T(8,128)S(1)}, f32[16,128]{1,0:T(8,128)S(1)}) conditional(s32[]{:T(128)} %convert_element_type.45, () %tuple.69, (s32[]{:T(128)}, bf16[1,512,128]{2,1,0:T(8,128)(2,1)S(1)}, bf16[16,128,128]{2,1,0:T(8,128)(2,1)}, bf16[1,512,128]{2,1,0:T(8,128)(2,1)S(1)}) %tuple.70), branch_computations={%region_5.6_spmd, %region_6.8_spmd} | conditional | flops 543225984 | bytes 10429472 | solution.py:137
  22.7 2.2 %fusion.4 = (f32[16,128]{1,0:T(8,128)S(1)}, f32[16,128,512]{2,1,0:T(8,128)S(1)}) fusion(pred[128,512]{1,0:T(8,128)(4,1)S(1)} %iota_compare_fusion, bf16[16,128,128]{2,1,0:T(8,128)(2,1)} %get-tuple-element.204, bf16[1,512,128]{2,1,0:T(8,128)(2,1)S(1)} %get-tuple-element.205), kind=kOutput, calls=%fused_computation.8 | convolution fusion | flops 271579136 | bytes 4923392 | tf_op jit(solution)/shard_map/cond/branch_1_fun/hid,jd->hij/dot_general | solution.py:39
  24.9 0.8 fusion.6
  26.3 3.2 %collective-permute-start = (bf16[16,128,128]{1,2,0:T(8,128)(2,1)S(1)}, bf16[16,128,128]{1,2,0:T(8,128)(2,1)S(1)}, u32[]{:S(2)}, u32[]{:S(2)}) collective-permute-start(bf16[16,128,128]{1,2,0:T(8,128)(2,1)S(1)} %copy.31), channel_id=1, source_target_pairs={{0,16},{1,17},{2,18},{3,19},{4,20},{5,21},{6,22},{7,23},{8,24},{9,... | collective-permute-start | bytes 1572872 | tf_op jit(solution)/shard_map/ppermute | solution.py:26
  29.5 2.1 %convert_element_type.39 = f32[16,128,128]{2,1,0:T(8,128)} convert(bf16[16,128,128]{2,1,0:T(8,128)(2,1)} %param.18) | non-fusion elementwise | flops 262144 | bytes 1572864 | tf_op jit(solution)/shard_map/convert_element_type | solution.py:68
  31.7 5.5 %all-gather.1 = f32[64,128]{1,0:T(8,128)S(1)} all-gather(f32[16,128]{1,0:T(8,128)S(1)} %get-tuple-element.246), channel_id=3, replica_groups=mesh['grp'=2,'head'=4,'seq'=4] {'seq'}, dimensions={0}, use_global_device_ids=true | all-gather | bytes 40960 | tf_op jit(solution)/shard_map/all_gather | solution.py:11
  37.1 13.6 %all-gather.7.cloned.1.call-done = f32[64,128,128]{2,1,0:T(8,128)} async-done(((f32[16,128,128]{2,1,0:T(8,128)}), f32[64,128,128]{2,1,0:T(8,128)}) %all-gather.7.cloned.1.call-update) | async-done | bytes 4194320 | tf_op jit(solution)/shard_map/all_gather | solution.py:11
  50.9 2.2 %conditional.8 = (f32[16,128,128]{1,2,0:T(8,128)}, f32[16,128,128]{2,1,0:T(8,128)}, f32[16,128]{1,0:T(8,128)S(1)}) conditional(s32[]{:T(128)} %convert_element_type.38, () %tuple.64, (f32[16,128,128]{2,1,0:T(8,128)}, f32[16,128,128]{2,1,0:T(8,128)S(1)}, f32[128,128]{1,0:T(8,128)S(1)}, s32[128,128]{1,0:T(8,128)S(1)}, s32[128,128]{1,0:T(8,128)S(1)}, ...), branch_computations={%region_10.11_spmd, %region_11.14_spmd} | conditional | flops 4846589952 | bytes 56656008 | solution.py:114
  50.9 1.1 broadcast.62
  52.0 1.1 broadcast.62.clone
  53.2 8.3 %all-gather.3 = f32[64,128]{1,0:T(8,128)S(1)} all-gather(f32[16,128]{1,0:T(8,128)S(1)} %get-tuple-element.252), channel_id=5, replica_groups=mesh['grp'=2,'head'=4,'seq'=4] {'seq'}, dimensions={0}, use_global_device_ids=true | all-gather | bytes 40960 | tf_op jit(solution)/shard_map/all_gather | solution.py:11
  61.5 59.6 %all-gather.9.cloned.1.call-done = f32[64,128,128]{2,1,0:T(8,128)} async-done(((f32[16,128,128]{2,1,0:T(8,128)}), f32[64,128,128]{2,1,0:T(8,128)}) %all-gather.9.cloned.1.call-update) | async-done | bytes 4194320 | tf_op jit(solution)/shard_map/all_gather | solution.py:11
  121.2 4.6 %while.27 = (s32[]{:T(128)}, f32[16,128,128]{2,1,0:T(8,128)S(1)}, f32[16,128]{1,0:T(8,128)S(1)}, s32[]{:T(128)}, f32[4,16,128,128]{3,2,1,0:T(8,128)}, /*index=5*...) while((s32[]{:T(128)}, f32[16,128,128]{2,1,0:T(8,128)S(1)}, ...), condition=%wide.region_15.16_spmd, body=%wide.region_14.15_spmd.sunk | while | flops 264198 | bytes 3170459 | solution.py:20
  121.2 1.5 bitcast_add_fusion.10
  122.8 1.5 bitcast_add_fusion.10
  124.3 1.5 bitcast_add_fusion.10
  125.9 1.3 copy.34
  127.3 41.0 %reduce-scatter.2.cloned.1.call-done = f32[16,16,128]{2,1,0:T(8,128)} async-done(((f32[16,128,128]{2,1,0:T(8,128)}), f32[16,16,128]{2,1,0:T(8,128)}) %reduce-scatter.2.cloned.1.call-update) | async-done | bytes 131088 | tf_op jit(solution)/shard_map/reduce_scatter | solution.py:145
  (33 shorter events, 1.9 us)
Async XLA Ops:
  6.5 3.9 %copy-start.3 = (bf16[1,128,128]{2,1,0:T(8,128)(2,1)S(1)}, bf16[1,128,128]{2,1,0:T(8,128)(2,1)}, u32[]{:S(2)}) copy-start(bf16[1,128,128]{2,1,0:T(8,128)(2,1)} %param.19) | copy-start | bytes 98308
  6.5 44.2 %all-gather.7.cloned.1.call-start = ((), (), s32[]{:S(2)}) async-start(), calls=%async_computation.2 | async-start | bytes 5242880 | tf_op jit(solution)/shard_map/all_gather | solution.py:11
  6.5 10.4 %copy-start.4 = (bf16[1,128,128]{2,1,0:T(8,128)(2,1)S(1)}, bf16[1,128,128]{2,1,0:T(8,128)(2,1)}, u32[]{:S(2)}) copy-start(bf16[1,128,128]{2,1,0:T(8,128)(2,1)} %param.20) | copy-start | bytes 98308
  9.3 1.0 copy-start.2
  10.4 110.7 %all-gather.9.cloned.1.call-start = ((), (), s32[]{:S(2)}) async-start(), calls=%async_computation.3 | async-start | bytes 5242880 | tf_op jit(solution)/shard_map/all_gather | solution.py:11
  26.3 24.5 %collective-permute-start = (bf16[16,128,128]{1,2,0:T(8,128)(2,1)S(1)}, bf16[16,128,128]{1,2,0:T(8,128)(2,1)S(1)}, u32[]{:S(2)}, u32[]{:S(2)}) collective-permute-start(bf16[16,128,128]{1,2,0:T(8,128)(2,1)S(1)} %copy.31), channel_id=1, source_target_pairs={{0,16},{1,17},{2,18},{3,19},{4,20},{5,21},{6,22},{7,23},{8,24},{9,... | collective-permute-start | bytes 1572872 | tf_op jit(solution)/shard_map/ppermute | solution.py:26
  53.1 115.2 %reduce-scatter.2.cloned.1.call-start = ((), (), s32[]{:S(2)}) async-start(), calls=%async_computation.1 | async-start | bytes 1179648 | tf_op jit(solution)/shard_map/reduce_scatter | solution.py:145
Sparse Core Ops, SparseCore 0:
  10.5 40.1 all-gather.6
  53.2 67.7 all-gather.8
  127.4 40.8 reduce-scatter.1
where the time goes:
time: 175 us
  waiting for transfers between devices  114 us (65%)
  blocking collectives  25.9 us (15%)
  between operations  13.3 us (8%)
  other arithmetic  9.76 us (6%)
  local copies, waits for them, and re-layouts  5.22 us (3%)
  starting transfers between devices  3.28 us (2%)
  matrix products  2.98 us (2%)
    all_gather x2, waiting for transfers between devices, prefix(): gathered = jax.tree.map(lambda a: lax.all_gather(a, axis), part)  73.2 us
    reduce_scatter x1, waiting for transfers between devices, per_device(): lax.psum_scatter(grad_term, ('grp', 'seq'), scatter_dimension=1, tiled=True)  41 us
    all_gather x2, blocking collectives, prefix(): gathered = jax.tree.map(lambda a: lax.all_gather(a, axis), part)  13.8 us
    all_gather x1, blocking collectives, per_device(): lax.all_gather(keys, 'seq', axis=1, tiled=True)  6.54 us
    all_gather x1, blocking collectives, per_device(): lax.all_gather(values, 'seq', axis=1, tiled=True)  5.58 us
    add x6, other arithmetic, add_pair(): return (earlier[0] + later[0], earlier[1] + later[1])  4.5 us
  transfers between devices with their start and end apart: 4, of which 3 were waited for; matrix products, arithmetic and copies ran while one was open for 3% of the time, Pallas kernels for 0%

commit v1 on v0

v1 whole, which is shorter than its diff:
```python
import functools

import jax
import jax.numpy as jnp
from jax import lax
from jax.experimental import pallas as pl
from jax.experimental.pallas import tpu as pltpu
from jax.sharding import PartitionSpec as P

F32 = jnp.float32
BF16 = jnp.bfloat16
NN = (((1,), (0,)), ((), ()))
NT = (((1,), (1,)), ((), ()))
TN = (((0,), (0,)), ((), ()))


def mm(a, b, dims=NN):
    return lax.dot_general(a, b, dims, preferred_element_type=F32)


def split(x):
    high = x.astype(BF16)
    return high, (x - high.astype(F32)).astype(BF16)


def cat(parts, axis):
    return jnp.concatenate(parts, axis)


def body(total, place, q_own, q_pair, w_ref, kv_own, kv_pair, hop_own, hop_pair, out, step):
    tokens, dh = q_own.shape[-2:]
    rows = 2 * tokens
    core, chip = place[0], place[1]
    scale = 1.0 / (dh**0.5)
    ones = jnp.ones((rows, dh), BF16)

    def position(axis):
        index = lax.broadcasted_iota(jnp.int32, (rows, rows), axis)
        return jnp.where((index < tokens) == (core == 0), index % tokens, tokens + index % tokens)

    seen = position(1) <= position(0)
    key = cat([kv_own[0], kv_pair[0]], 0)
    value = cat([cat([kv_own[1], kv_pair[1]], 0), ones], 1)
    hops = hop_own.shape[0]

    def head(h):
        query = cat([q_own[h], q_pair[h]], 0)
        wmat = w_ref[h]
        phi_q = jnp.exp(mm(query, wmat))
        phi_k = jnp.exp(mm(key, wmat))
        qh, ql = split(phi_q)
        kh, kl = split(phi_k)
        p = jnp.where(seen, jnp.exp(mm(query, key, NT) * scale), 0.0)
        denom_t = jnp.sum(p, axis=1, keepdims=True)
        numer_t = mm(p.astype(BF16), value[:, :dh])
        a = jnp.where(seen, mm(cat([qh, ql, qh], 1), cat([kh, kh, kl], 1), NT), 0.0)
        ah, al = split(a)
        both = mm(cat([ah, al], 1), cat([value, value], 0))

        def earlier(hop, carry):
            state, numer_t, denom_t = carry
            live = hop < chip
            key_j = cat([hop_own[hop, 0], hop_pair[hop, 0]], 0)
            value_j = cat([cat([hop_own[hop, 1], hop_pair[hop, 1]], 0), ones], 1)
            p = jnp.where(live, jnp.exp(mm(query, key_j, NT) * scale), 0.0)
            denom_t = denom_t + jnp.sum(p, axis=1, keepdims=True)
            numer_t = numer_t + mm(p.astype(BF16), value_j[:, :dh])
            phi_j = jnp.where(live, jnp.exp(mm(key_j, wmat)), 0.0)
            jh, jl = split(phi_j)
            state = state + mm(cat([jh, jl], 0), cat([value_j, value_j], 0), TN)
            return state, numer_t, denom_t

        carry = (jnp.zeros((wmat.shape[1], 2 * dh), F32), numer_t, denom_t)
        if hops == 1:
            carry = earlier(0, carry)
        else:
            carry = lax.fori_loop(0, hops, earlier, carry)
        state, numer_t, denom_t = carry
        sh, sl = split(state)
        both = both + mm(cat([qh, ql, qh], 1), cat([sh, sh, sl], 0))
        target = (numer_t / denom_t).astype(BF16).astype(F32)
        inverse = 1.0 / both[:, dh:]
        student = both[:, :dh] * inverse
        cotangent = (student - target) * (2.0 / total) * inverse
        g = cat([cotangent, -cotangent * student], 1)
        gh, gl = split(g)
        da = jnp.where(seen, mm(cat([gh, gl], 1), cat([value, value], 1), NT), 0.0)
        dah, dal = split(da)
        wide_k = mm(dah, cat([kh, kl], 1))
        dphi_q = wide_k[:, :dh] + wide_k[:, dh:] + mm(dal, kh)
        dphi_q = dphi_q + mm(cat([gh, gl, gh], 1), cat([sh, sh, sl], 1), NT)
        wide_q = mm(dah, cat([qh, ql], 1), TN)
        dphi_k = wide_q[:, :dh] + wide_q[:, dh:] + mm(dal, qh, TN)
        zqh, zql = split(dphi_q * phi_q)
        zkh, zkl = split(dphi_k * phi_k)
        wide = mm(cat([query, key], 0), cat([cat([zqh, zql], 1), cat([zkh, zkl], 1)], 0), TN)
        grad = wide[:, : wmat.shape[1]] + wide[:, wmat.shape[1] :]
        ds = mm(cat([qh, qh, ql], 0), cat([gh, gl, gh], 0), TN)
        dsh, dsl = split(ds)

        def back(hop, grad):
            live = hop < chip
            key_j = cat([hop_own[hop, 0], hop_pair[hop, 0]], 0)
            value_j = cat([cat([hop_own[hop, 1], hop_pair[hop, 1]], 0), ones], 1)
            phi_j = jnp.where(live, jnp.exp(mm(key_j, wmat)), 0.0)
            dphi_j = mm(cat([value_j, value_j], 1), cat([dsh, dsl], 1), NT)
            zh, zl = split(dphi_j * phi_j)
            wide = mm(key_j, cat([zh, zl], 1), TN)
            return grad + wide[:, : wmat.shape[1]] + wide[:, wmat.shape[1] :]

        if hops == 1:
            grad = back(0, grad)
        else:
            grad = lax.fori_loop(0, hops, back, grad)
        out[h] = grad

    heads = w_ref.shape[0]

    def group(i, _):
        for j in range(step):
            head(i * step + j)
        return 0

    lax.fori_loop(0, heads // step, group, 0)


def gradients(place, q_own, q_pair, wmat, kv_own, kv_pair, hop_own, hop_pair, total, step=2):
    vmem = pl.BlockSpec(memory_space=pltpu.VMEM)
    return pl.pallas_call(
        lambda *refs: body(total, *refs, step),
        in_specs=[pl.BlockSpec(memory_space=pltpu.SMEM)] + [vmem] * 7,
        out_specs=vmem,
        out_shape=jax.ShapeDtypeStruct(wmat.shape, F32),
        name="gradients",
    )(place, q_own, q_pair, wmat, kv_own, kv_pair, hop_own, hop_pair)


def per_device(queries, keys, values, feature_map):
    count = lax.axis_size("seq")
    groups = lax.axis_size("grp")
    chips = count // 2
    seq = lax.axis_index("seq")
    core, chip = seq % 2, seq // 2
    total = keys.shape[1] * count
    heads = queries.shape[0] // 2
    kv = cat([keys, values], 0)
    swap = [(i, i ^ 1) for i in range(count)]
    hop_own = jnp.stack(
        [
            lax.ppermute(kv, "seq", [(i, i + 2 * k) for i in range(count - 2 * k)])
            for k in range(1, chips)
        ]
    )
    halves = queries.reshape(2, heads, *queries.shape[1:])
    q_own = lax.dynamic_index_in_dim(halves, core, 0, False)
    q_pair = lax.ppermute(lax.dynamic_index_in_dim(halves, 1 - core, 0, False), "seq", swap)
    kv_pair = lax.ppermute(kv, "seq", swap)
    hop_pair = lax.ppermute(hop_own, "seq", swap)
    wmat = lax.dynamic_slice_in_dim(feature_map, core * heads, heads, 0)
    place = jnp.stack([core, chip]).astype(jnp.int32)
    grad = gradients(place, q_own, q_pair, wmat, kv, kv_pair, hop_own, hop_pair, total)
    mine = wmat.shape[1] // groups
    grad = lax.dynamic_slice_in_dim(grad, lax.axis_index("grp") * mine, mine, 1)
    grad = grad.reshape(heads, chips, 2, mine // count, grad.shape[-1])
    away = lax.ppermute(lax.dynamic_index_in_dim(grad, 1 - core, 2, False), "seq", swap)
    stay = lax.dynamic_index_in_dim(grad, core, 2, False)
    first = core == 0
    part = cat([jnp.where(first, stay, away), jnp.where(first, away, stay)], 0)
    result = lax.dynamic_index_in_dim(part, chip, 1, False)
    for k in range(1, chips):
        send = lax.dynamic_index_in_dim(part, (chip + k) % chips, 1, False)
        ring = [(i, (i + 2 * k) % count) for i in range(count)]
        result = result + lax.ppermute(send, "seq", ring)
    return result


def solution(mesh):
    return jax.shard_map(
        per_device,
        mesh=mesh,
        in_specs=(
            P("head", "seq", None),
            P("head", "seq", None),
            P("head", "seq", None),
            P("head", None, None),
        ),
        out_specs=P("head", ("grp", "seq"), None),
        check_vma=False,
    )
```

time: 175 us -> 39.1 us (0.22)
  waiting for transfers between devices: 114 us -> 6.69 us
  blocking collectives: 25.9 us -> 0 us
  Pallas kernels: 0 us -> 18 us
  between operations: 13.3 us -> 0.11 us
  other arithmetic: 9.76 us -> 1.3 us
  starting transfers between devices: 3.28 us -> 8.12 us
  matrix products: 2.98 us -> 0 us
    all_gather x2 -> x0, waiting for transfers between devices: 73.2 us -> none  [prefix(): gathered = jax.tree.map(lambda a: lax.all_gather(a, axis), part)]
    reduce_scatter x1 -> x0, waiting for transfers between devices: 41 us -> none  [per_device(): lax.psum_scatter(grad_term, ('grp', 'seq'), scatter_dimension=1, tiled=True)]
    all_gather x4 -> x0, blocking collectives: 25.9 us -> none  [the longest x2 13.8 us: prefix(): gathered = jax.tree.map(lambda a: lax.all_gather(a, axis), part)]
    pallas_call x0 -> x1, Pallas kernels: none -> 18 us  [gradients(): pl.pallas_call(lambda *refs: body(total, *refs, step), in_specs=[pl.Block...]
    ppermute x1 -> x6, waiting for transfers between devices: 0.01 us -> 6.69 us  [the longest x1 3.82 us: per_device(): result = result + lax.ppermute(send, 'seq', ring)]
    convert_element_type x5 -> x0, other arithmetic: 5.15 us -> none  [the longest x1 2.13 us: student_part(): query_rows = queries.astype(jnp.float32)]
    ppermute x1 -> x6, starting transfers between devices: 3.2 us -> 8.12 us  [the longest x1 4.9 us: per_device(): lax.ppermute(kv, 'seq', [(i, i + 2 * k) for i in range(count - 2 * k)])]
    add x7 -> x1, other arithmetic: 4.5 us -> 0.67 us  [per_device(): result = result + lax.ppermute(send, 'seq', ring)]
  transfers between devices with their start and end apart: 4 -> 6, of which waited for: 3 -> 4; matrix products, arithmetic and copies ran while one was open for 3% -> 3% of each run, Pallas kernels for 0% -> 0%
where the time goes in v1:
time: 39.1 us; the launch traced here: 38.8 us
  Pallas kernels  18 us (46%)
  starting transfers between devices  8.12 us (21%)
  waiting for transfers between devices  6.69 us (17%)
  local copies, waits for them, and re-layouts  4.6 us (12%)
  other arithmetic  1.3 us (3%)
    pallas_call x1, Pallas kernels, gradients(): pl.pallas_call(lambda *refs: body(total, *refs, step), in_specs=[pl.Block...  18 us
    ppermute x1, starting transfers between devices, per_device(): lax.ppermute(kv, 'seq', [(i, i + 2 * k) for i in range(count - 2 * k)])  4.9 us
    ppermute x1, waiting for transfers between devices, per_device(): result = result + lax.ppermute(send, 'seq', ring)  3.82 us
    ppermute x1, starting transfers between devices, per_device(): result = result + lax.ppermute(send, 'seq', ring)  2.43 us
    squeeze x1, local copies, waits for them, and re-layouts, per_device(): lax.dynamic_index_in_dim(halves, 1 - core, 0, False)  1.85 us
    ppermute x1, waiting for transfers between devices, per_device(): lax.ppermute(lax.dynamic_index_in_dim(grad, 1 - core, 2, False), 'seq', s...  1.19 us
    ppermute x1, waiting for transfers between devices, per_device(): lax.ppermute(kv, 'seq', [(i, i + 2 * k) for i in range(count - 2 * k)])  1.02 us
    unnamed x17, local copies, waits for them, and re-layouts  0.98 us
  transfers between devices with their start and end apart: 6, of which 4 were waited for; matrix products, arithmetic and copies ran while one was open for 3% of the time, Pallas kernels for 0%

profile of v1, /device:TPU:0, one launch (start us, length us, event | category | flops | bytes accessed | tf_op | source)
XLA Modules:
  0.0 38.8 jit_solution(5505701851519615612)
XLA Ops:
  0.0 0.0 copy-start
  0.0 1.8 %dynamic-slice_bitcast_fusion = (bf16[8,128,128]{2,1,0:T(8,128)(2,1)S(1)}, bf16[8,128,128]{2,1,0:T(8,128)(2,1)}) fusion(bf16[2,8,128,128]{3,2,1,0:T(8,128)(2,1)} %bitcast.22, s32[]{:T(128)S(6)} %select_n.54, s32[]{:T(128)S(6)} %select_n.53), kind=kLoop, calls=%fused_computation.4 | loop fusion | bytes 1048584 | tf_op jit(solution)/shard_map/jit(dynamic_index_in_dim)/squeeze | solution.py:156
  1.9 0.5 %collective-permute-start = (bf16[8,128,128]{2,1,0:T(8,128)(2,1)S(1)}, bf16[8,128,128]{2,1,0:T(8,128)(2,1)S(1)}, u32[]{:S(2)}, u32[]{:S(2)}) collective-permute-start(bf16[8,128,128]{2,1,0:T(8,128)(2,1)S(1)} %get-tuple-element.5), channel_id=1, source_target_pairs={{0,1},{1,0},{2,3},{3,2},{4,5},{5,4},{6,7},{7,6},{8,9},{9,8},{10,11... | collective-permute-start | bytes 786440 | tf_op jit(solution)/shard_map/ppermute | solution.py:156
  2.4 0.0 copy-done.6
  2.4 0.3 copy-done.7
  2.6 4.9 %collective-permute-start.2 = (bf16[2,128,128]{2,1,0:T(8,128)(2,1)S(1)}, bf16[2,128,128]{2,1,0:T(8,128)(2,1)S(1)}, u32[]{:S(2)}, u32[]{:S(2)}) collective-permute-start(bf16[2,128,128]{2,1,0:T(8,128)(2,1)S(1)} %constant_dynamic-update-slice_fusion.refs_4_), channel_id=1, source_target_pairs={{0,2},{1,3},{4,6},{5,7},{8,10},{9,11},{12,14},{13,15},{16,18},{17,... | collective-permute-start | bytes 196616 | tf_op jit(solution)/shard_map/ppermute | solution.py:150
  7.5 0.1 collective-permute-start.1
  7.6 0.0 copy-done
  7.7 0.7 %constant_dynamic-slice_fusion.3.refs_3_ = bf16[8,128,128]{2,1,0:T(8,128)(2,1)} fusion(bf16[16,128,128]{2,1,0:T(8,128)(2,1)S(1)} %copy-done, s32[]{:T(128)S(6)} %select_n.55), kind=kLoop, calls=%fused_computation.19 | loop fusion | bytes 524292 | tf_op jit(solution)/shard_map/dynamic_slice | solution.py:159
  8.4 1.0 %collective-permute-done.2 = bf16[2,128,128]{2,1,0:T(8,128)(2,1)S(1)} collective-permute-done((bf16[2,128,128]{2,1,0:T(8,128)(2,1)S(1)}, bf16[2,128,128]{2,1,0:T(8,128)(2,1)S(1)}, u32[]{:S(2)}, u32[]{:S(2)}) %collective-permute-start.2) | collective-permute-done | bytes 65568 | tf_op jit(solution)/shard_map/ppermute | solution.py:150
  9.4 0.0 collective-permute-start.3
  9.4 0.6 %pad_add_fusion.refs_0_ = s32[2]{0:T(128)} fusion(s32[1]{0:T(128)} %bitcast.1, s32[1]{0:T(128)} %bitcast), kind=kLoop, calls=%fused_computation.20 | loop fusion | flops 2 | bytes 16 | tf_op jit(solution)/shard_map/stack | solution.py:160
  10.0 0.0 collective-permute-done.1.refs_5_
  10.0 0.7 %collective-permute-done.3.refs_7_ = bf16[1,2,128,128]{3,2,1,0:T(8,128)(2,1)S(1)} collective-permute-done((bf16[1,2,128,128]{3,2,1,0:T(8,128)(2,1)S(1)}, bf16[1,2,128,128]{3,2,1,0:T(8,128)(2,1)S(1)}, u32[]{:S(2)}, u32[]{:S(2)}) %collective-permute-start.3) | collective-permute-done | bytes 65568 | tf_op jit(solution)/shard_map/ppermute | solution.py:158
  10.7 0.0 collective-permute-done.refs_2_
  10.7 0.6 %copy-done.5 = bf16[1,2,128,128]{3,2,1,0:T(8,128)(2,1)} copy-done((bf16[1,2,128,128]{3,2,1,0:T(8,128)(2,1)}, bf16[1,2,128,128]{3,2,1,0:T(8,128)(2,1)S(1)}, u32[]{:S(2)}) %copy-start.5) | copy-done | bytes 65560
  11.3 0.1 copy-done.1
  11.4 18.0 %gradients.1 = f32[8,128,128]{2,1,0:T(8,128)} custom-call(s32[2]{0:T(128)} %pad_add_fusion.refs_0_, bf16[8,128,128]{2,1,0:T(8,128)(2,1)} %get-tuple-element.6.refs_1_, bf16[8,128,128]{2,1,0:T(8,128)(2,1)} %copy-done.1, bf16[8,128,128]{2,1,0:T(8,128)(2,1)} %constant_dynamic-slice_fusion.3.refs_3_, bf16[2,128,128]{2,1,0:T(8,128)(2,1)} %copy-done.2, ...), custom_call_target="tpu_custom_call" | custom-call | tf_op jit(solution)/shard_map/gradients/pallas_call | solution.py:129
  29.4 1.0 %constant_dynamic-slice_fusion.2 = f32[8,64,128]{2,1,0:T(8,128)S(1)} fusion(f32[8,128,128]{2,1,0:T(8,128)} %gradients.1, s32[]{:T(128)S(6)} %select_n.56), kind=kLoop, calls=%fused_computation.18 | loop fusion | bytes 524292 | tf_op jit(solution)/shard_map/dynamic_slice | solution.py:163
  30.4 0.2 collective-permute-start.4
  30.6 1.2 %collective-permute-done.4 = f32[8,2,16,128]{3,2,0,1:T(8,128)S(1)} collective-permute-done((f32[8,2,16,128]{3,2,0,1:T(8,128)S(1)}, f32[8,2,16,128]{3,2,0,1:T(8,128)S(1)}, u32[]{:S(2)}, u32[]{:S(2)}) %collective-permute-start.4) | collective-permute-done | bytes 131104 | tf_op jit(solution)/shard_map/ppermute | solution.py:165
  31.9 2.4 %collective-permute-start.5 = (f32[16,16,128]{2,1,0:T(8,128)S(1)}, f32[16,16,128]{2,1,0:T(8,128)S(1)}, u32[]{:S(2)}, u32[]{:S(2)}) collective-permute-start(f32[16,16,128]{2,1,0:T(8,128)S(1)} %fusion.1), channel_id=1, source_target_pairs={{0,2},{1,3},{2,0},{3,1},{4,6},{5,7},{6,4},{7,5},{8,10},{9,11},{10,... | collective-permute-start | bytes 393224 | tf_op jit(solution)/shard_map/ppermute | solution.py:173
  34.3 3.8 %collective-permute-done.5 = f32[16,16,128]{2,1,0:T(8,128)S(1)} collective-permute-done((f32[16,16,128]{2,1,0:T(8,128)S(1)}, f32[16,16,128]{2,1,0:T(8,128)S(1)}, u32[]{:S(2)}, u32[]{:S(2)}) %collective-permute-start.5) | collective-permute-done | bytes 131104 | tf_op jit(solution)/shard_map/ppermute | solution.py:173
  38.1 0.7 %fusion.4 = f32[16,16,128]{2,1,0:T(8,128)} fusion(f32[16,16,128]{2,1,0:T(8,128)S(1)} %collective-permute-done.5, s32[]{:T(128)S(6)} %select_n.59, f32[8,2,16,128]{3,2,0,1:T(8,128)S(1)} %get-tuple-element.8, f32[8,2,16,128]{3,2,0,1:T(8,128)S(1)} %get-tuple-element.7), kind=kLoop, calls=%fused_computation.10 | loop fusion | flops 65536 | bytes 524292 | tf_op jit(solution)/shard_map/add | solution.py:173
  (16 shorter events, 0.1 us)
Async XLA Ops:
  0.0 7.6 %copy-start = (bf16[16,128,128]{2,1,0:T(8,128)(2,1)S(1)}, bf16[16,128,128]{2,1,0:T(8,128)(2,1)}, u32[]{:S(2)}) copy-start(bf16[16,128,128]{2,1,0:T(8,128)(2,1)} %param.7) | copy-start | bytes 1572868
  0.0 2.3 %copy-start.6 = (bf16[1,128,128]{2,1,0:T(8,128)(2,1)S(1)}, bf16[1,128,128]{2,1,0:T(8,128)(2,1)}, u32[]{:S(2)}) copy-start(bf16[1,128,128]{2,1,0:T(8,128)(2,1)} %param.5) | copy-start | bytes 98308
  1.9 0.8 %copy-start.7 = (bf16[1,128,128]{2,1,0:T(8,128)(2,1)S(1)}, bf16[1,128,128]{2,1,0:T(8,128)(2,1)}, u32[]{:S(2)}) copy-start(bf16[1,128,128]{2,1,0:T(8,128)(2,1)} %param.6) | copy-start | bytes 98308
  1.9 8.8 %collective-permute-start = (bf16[8,128,128]{2,1,0:T(8,128)(2,1)S(1)}, bf16[8,128,128]{2,1,0:T(8,128)(2,1)S(1)}, u32[]{:S(2)}, u32[]{:S(2)}) collective-permute-start(bf16[8,128,128]{2,1,0:T(8,128)(2,1)S(1)} %get-tuple-element.5), channel_id=1, source_target_pairs={{0,1},{1,0},{2,3},{3,2},{4,5},{5,4},{6,7},{7,6},{8,9},{9,8},{10,11... | collective-permute-start | bytes 786440 | tf_op jit(solution)/shard_map/ppermute | solution.py:156
  2.6 5.8 %copy-start.2 = (bf16[2,128,128]{2,1,0:T(8,128)(2,1)}, bf16[2,128,128]{2,1,0:T(8,128)(2,1)S(1)}, u32[]{:S(2)}) copy-start(bf16[2,128,128]{2,1,0:T(8,128)(2,1)S(1)} %constant_dynamic-update-slice_fusion.refs_4_) | copy-start | bytes 196612
  2.6 6.8 %collective-permute-start.2 = (bf16[2,128,128]{2,1,0:T(8,128)(2,1)S(1)}, bf16[2,128,128]{2,1,0:T(8,128)(2,1)S(1)}, u32[]{:S(2)}, u32[]{:S(2)}) collective-permute-start(bf16[2,128,128]{2,1,0:T(8,128)(2,1)S(1)} %constant_dynamic-update-slice_fusion.refs_4_), channel_id=1, source_target_pairs={{0,2},{1,3},{4,6},{5,7},{8,10},{9,11},{12,14},{13,15},{16,18},{17,... | collective-permute-start | bytes 196616 | tf_op jit(solution)/shard_map/ppermute | solution.py:150
  7.5 2.5 %collective-permute-start.1 = (bf16[2,128,128]{2,1,0:T(8,128)(2,1)S(1)}, bf16[2,128,128]{2,1,0:T(8,128)(2,1)S(1)}, u32[]{:S(2)}, u32[]{:S(2)}) collective-permute-start(bf16[2,128,128]{2,1,0:T(8,128)(2,1)S(1)} %constant_dynamic-update-slice_fusion.refs_4_), channel_id=1, source_target_pairs={{0,1},{1,0},{2,3},{3,2},{4,5},{5,4},{6,7},{7,6},{8,9},{9,8},{10,11... | collective-permute-start | bytes 196616 | tf_op jit(solution)/shard_map/ppermute | solution.py:157
  9.4 1.3 %copy-start.3 = (bf16[2,128,128]{2,1,0:T(8,128)(2,1)}, bf16[2,128,128]{2,1,0:T(8,128)(2,1)S(1)}, u32[]{:S(2)}) copy-start(bf16[2,128,128]{2,1,0:T(8,128)(2,1)S(1)} %collective-permute-done.2) | copy-start | bytes 196612
  9.4 1.3 %collective-permute-start.3 = (bf16[1,2,128,128]{3,2,1,0:T(8,128)(2,1)S(1)}, bf16[1,2,128,128]{3,2,1,0:T(8,128)(2,1)S(1)}, u32[]{:S(2)}, u32[]{:S(2)}) collective-permute-start(bf16[1,2,128,128]{3,2,1,0:T(8,128)(2,1)S(1)} %bitcast.24), channel_id=1, source_target_pairs={{0,1},{1,0},{2,3},{3,2},{4,5},{5,4},{6,7},{7,6},{8,9},{9,8},{10,11... | collective-permute-start | bytes 196616 | tf_op jit(solution)/shard_map/ppermute | solution.py:158
  10.0 0.7 %copy-start.4 = (bf16[2,128,128]{2,1,0:T(8,128)(2,1)}, bf16[2,128,128]{2,1,0:T(8,128)(2,1)S(1)}, u32[]{:S(2)}) copy-start(bf16[2,128,128]{2,1,0:T(8,128)(2,1)S(1)} %collective-permute-done.1.refs_5_) | copy-start | bytes 196612
  10.7 0.6 %copy-start.5 = (bf16[1,2,128,128]{3,2,1,0:T(8,128)(2,1)}, bf16[1,2,128,128]{3,2,1,0:T(8,128)(2,1)S(1)}, u32[]{:S(2)}) copy-start(bf16[1,2,128,128]{3,2,1,0:T(8,128)(2,1)S(1)} %collective-permute-done.3.refs_7_) | copy-start | bytes 196612
  10.7 0.7 %copy-start.1 = (bf16[8,128,128]{2,1,0:T(8,128)(2,1)}, bf16[8,128,128]{2,1,0:T(8,128)(2,1)S(1)}, u32[]{:S(2)}) copy-start(bf16[8,128,128]{2,1,0:T(8,128)(2,1)S(1)} %collective-permute-done.refs_2_) | copy-start | bytes 786436
  30.4 1.4 %collective-permute-start.4 = (f32[8,2,16,128]{3,2,0,1:T(8,128)S(1)}, f32[8,2,16,128]{3,2,0,1:T(8,128)S(1)}, u32[]{:S(2)}, u32[]{:S(2)}) collective-permute-start(f32[8,2,16,128]{3,2,0,1:T(8,128)S(1)} %bitcast.23), channel_id=1, source_target_pairs={{0,1},{1,0},{2,3},{3,2},{4,5},{5,4},{6,7},{7,6},{8,9},{9,8},{10,11... | collective-permute-start | bytes 393224 | tf_op jit(solution)/shard_map/ppermute | solution.py:165
  31.9 6.2 %collective-permute-start.5 = (f32[16,16,128]{2,1,0:T(8,128)S(1)}, f32[16,16,128]{2,1,0:T(8,128)S(1)}, u32[]{:S(2)}, u32[]{:S(2)}) collective-permute-start(f32[16,16,128]{2,1,0:T(8,128)S(1)} %fusion.1), channel_id=1, source_target_pairs={{0,2},{1,3},{2,0},{3,1},{4,6},{5,7},{6,4},{7,5},{8,10},{9,11},{10,... | collective-permute-start | bytes 393224 | tf_op jit(solution)/shard_map/ppermute | solution.py:173

commit v2 on v1

v2 whole, which is shorter than its diff:
```python
import jax
import jax.numpy as jnp
from jax import lax
from jax.experimental import pallas as pl
from jax.experimental.pallas import tpu as pltpu
from jax.sharding import PartitionSpec as P

F32 = jnp.float32
BF16 = jnp.bfloat16
WIRE = BF16
NN = (((1,), (0,)), ((), ()))
NT = (((1,), (1,)), ((), ()))
TN = (((0,), (0,)), ((), ()))


def mm(a, b, dims=NN):
    return lax.dot_general(a, b, dims, preferred_element_type=F32)


def split(x):
    high = x.astype(BF16)
    return high, (x - high.astype(F32)).astype(BF16)


def cat(parts, axis):
    return jnp.concatenate(parts, axis)


def interleave(make, heads, step):
    def group(i, _):
        running = [make(i * step + j) for j in range(step)]
        while running:
            running = [r for r in running if next(r, True) is None]
        return 0

    lax.fori_loop(0, heads // step, group, 0)


def extended(value):
    return cat([value, jnp.ones(value.shape, BF16)], 1)


def own_block(core, kv_own, kv_pair):
    tokens = kv_own.shape[1]
    rows = 2 * tokens

    def position(axis):
        index = lax.broadcasted_iota(jnp.int32, (rows, rows), axis)
        return jnp.where((index < tokens) == (core == 0), index % tokens, tokens + index % tokens)

    key = cat([kv_own[0], kv_pair[0]], 0)
    value = extended(cat([kv_own[1], kv_pair[1]], 0))
    return position(1) <= position(0), key, value


def cotangents(total, numer_t, denom_t, both):
    dh = numer_t.shape[1]
    target = (numer_t / denom_t).astype(BF16).astype(F32)
    inverse = 1.0 / both[:, dh:]
    student = both[:, :dh] * inverse
    g = ((student - target) * (2.0 / total) * inverse).astype(BF16)
    return g, jnp.sum(g.astype(F32) * student, axis=1, keepdims=True)


def score_cotangent(seen, g, value, shift):
    return split(jnp.where(seen, mm(g, value[:, : g.shape[1]], NT) - shift, 0.0))


def map_gradient(query, key, dphi_q, phi_q, dphi_k, phi_k):
    zqh, zql = split(dphi_q * phi_q)
    zkh, zkl = split(dphi_k * phi_k)
    stacked = cat([cat([zqh, zql], 1), cat([zkh, zkl], 1)], 0)
    return mm(cat([query, key], 0), stacked, TN)


def first_body(step, place, q_own, q_pair, w_ref, kv_own, kv_pair, *outs):
    numer_ref, denom_ref, both_ref = outs
    dh = q_own.shape[-1]
    core = place[0]
    scale = 1.0 / (dh**0.5)
    seen, key, value = own_block(core, kv_own, kv_pair)
    heads = w_ref.shape[0]

    def forward(h):
        query = cat([q_own[h], q_pair[h]], 0)
        wmat = w_ref[h]
        phi_q = jnp.exp(mm(query, wmat))
        phi_k = jnp.exp(mm(key, wmat))
        qh, kh = phi_q.astype(BF16), phi_k.astype(BF16)
        yield
        p = jnp.where(seen, jnp.exp(mm(query, key, NT) * scale), 0.0)
        a = jnp.where(seen, mm(qh, kh, NT), 0.0)
        yield
        denom_ref[h] = jnp.sum(p, axis=1, keepdims=True)
        numer_ref[h] = mm(p.astype(BF16), value[:, :dh])
        both_ref[h] = mm(cat(split(a), 1), cat([value, value], 0))

    interleave(forward, heads, step)


def second_body(total, step, place, q_own, q_pair, w_ref, kv_own, kv_pair, *refs):
    numer_ref, denom_ref, both_ref, hop_own, hop_pair, grad_ref = refs
    dh = q_own.shape[-1]
    core, chip = place[0], place[1]
    scale = 1.0 / (dh**0.5)
    hops = hop_own.shape[0]
    heads, _, feats = w_ref.shape

    def hop_block(hop):
        key_j = cat([hop_own[hop, 0], hop_pair[hop, 0]], 0)
        return key_j, extended(cat([hop_own[hop, 1], hop_pair[hop, 1]], 0))

    def loop(function, carry):
        return function(0, carry) if hops == 1 else lax.fori_loop(0, chip, function, carry)

    def whole(h):
        seen, key, value = own_block(core, kv_own, kv_pair)
        query = cat([q_own[h], q_pair[h]], 0)
        wmat = w_ref[h]

        def earlier(hop, carry):
            state, total_j, numer_t, denom_t = carry
            key_j, value_j = hop_block(hop)
            p = jnp.exp(mm(query, key_j, NT) * scale)
            denom_t = denom_t + jnp.sum(p, axis=1, keepdims=True)
            numer_t = numer_t + mm(p.astype(BF16), value_j[:, :dh])
            phi_j = jnp.exp(mm(key_j, wmat)).astype(BF16)
            state = state + mm(phi_j, value_j, TN)
            total_j = total_j + jnp.sum(phi_j.astype(F32), axis=0, keepdims=True)
            return state, total_j, numer_t, denom_t

        empty = (jnp.zeros((feats, 2 * dh), F32), jnp.zeros((1, feats), F32))
        state, total_j, numer_t, denom_t = loop(earlier, empty + (numer_ref[h], denom_ref[h]))
        phi_q, phi_k = jnp.exp(mm(query, wmat)), jnp.exp(mm(key, wmat))
        yield
        qh, kh = phi_q.astype(BF16), phi_k.astype(BF16)
        sh, sl = split(state)
        both = both_ref[h] + mm(cat([qh, qh], 1), cat([sh, sl], 0))
        yield
        g, shift = cotangents(total, numer_t, denom_t, both)
        yield
        da, dal = score_cotangent(seen, g, value, shift)
        yield
        dphi_q = mm(cat([da, dal], 1), cat([kh, kh], 0)) - shift * total_j
        dphi_q = dphi_q + mm(cat([g, g], 1), cat([sh[:, :dh], sl[:, :dh]], 1), NT)
        dphi_k = mm(cat([da, dal], 0), cat([qh, qh], 0), TN)
        dsh, dsl = split(mm(qh, g, TN))
        lost = jnp.sum(qh.astype(F32) * shift, axis=0, keepdims=True)
        yield
        wide = map_gradient(query, key, dphi_q, phi_q, dphi_k, phi_k)
        yield

        def back(hop, wide):
            key_j, value_j = hop_block(hop)
            value_j = value_j[:, :dh]
            phi_j = jnp.exp(mm(key_j, wmat))
            dphi_j = mm(cat([value_j, value_j], 1), cat([dsh, dsl], 1), NT) - lost
            zh, zl = split(dphi_j * phi_j)
            return wide + mm(key_j, cat([zh, zl], 1), TN)

        wide = loop(back, wide)
        yield
        grad_ref[h] = wide[:, :feats] + wide[:, feats:]

    @pl.when(chip != 0)
    def _():
        interleave(whole, heads, step)

    def alone(h):
        seen, key, value = own_block(core, kv_own, kv_pair)
        query = cat([q_own[h], q_pair[h]], 0)
        phi_q, phi_k = jnp.exp(mm(query, w_ref[h])), jnp.exp(mm(key, w_ref[h]))
        qh, kh = phi_q.astype(BF16), phi_k.astype(BF16)
        g, shift = cotangents(total, numer_ref[h], denom_ref[h], both_ref[h])
        yield
        da, dal = score_cotangent(seen, g, value, shift)
        yield
        dphi_q = mm(cat([da, dal], 1), cat([kh, kh], 0))
        dphi_k = mm(cat([da, dal], 0), cat([qh, qh], 0), TN)
        yield
        wide = map_gradient(query, key, dphi_q, phi_q, dphi_k, phi_k)
        yield
        grad_ref[h] = wide[:, :feats] + wide[:, feats:]

    @pl.when(chip == 0)
    def _():
        interleave(alone, heads, step)


def call(function, outs, *operands):
    vmem = pl.BlockSpec(memory_space=pltpu.VMEM)
    return pl.pallas_call(
        function,
        in_specs=[pl.BlockSpec(memory_space=pltpu.SMEM)] + [vmem] * (len(operands) - 1),
        out_specs=[vmem] * len(outs),
        out_shape=[jax.ShapeDtypeStruct(s, F32) for s in outs],
        compiler_params=pltpu.CompilerParams(vmem_limit_bytes=16 << 20),
        cost_estimate=pl.CostEstimate(flops=2 * 10**9, bytes_accessed=10**7, transcendentals=10**6),
    )(*operands)


def per_device(queries, keys, values, feature_map):
    count, groups = lax.axis_size("seq"), lax.axis_size("grp")
    chips = count // 2
    seq, grp = lax.axis_index("seq"), lax.axis_index("grp")
    core, chip = seq & 1, seq >> 1
    tokens, dh = keys.shape[1:]
    total = tokens * count
    feats = feature_map.shape[2]
    hn = queries.shape[0] // (2 * groups)
    lines = dh // (groups * count)
    step = hn if hn <= 4 else 1
    swap = [(i, i ^ 1) for i in range(count)]

    def mine(array, half):
        split_heads = array.reshape(2 * groups, hn, *array.shape[1:])
        return lax.dynamic_index_in_dim(split_heads, half * groups + grp, 0, False)

    kv = cat([keys, values], 0)
    hops = []
    for k in range(1, chips):
        ring = [(i, (i + 2 * k) % count) for i in range(count)]
        hops.append(lax.ppermute(kv, "seq", ring))
    place = jnp.stack([core, chip]).astype(jnp.int32)
    kv_pair = lax.ppermute(kv, "seq", swap)
    q_pair = lax.ppermute(mine(queries, 1 - core), "seq", swap)
    local = (place, mine(queries, core), q_pair, mine(feature_map, core), kv, kv_pair)
    rows = 2 * tokens
    state = [(hn, rows, dh), (hn, rows, 1), (hn, rows, 2 * dh)]
    state = call(lambda *r: first_body(step, *r), state, *local)
    hop_own = jnp.stack(hops)
    hop_pair = lax.ppermute(hop_own, "seq", swap)
    (grad,) = call(
        lambda *r: second_body(total, step, *r),
        [(hn, dh, feats)],
        *local,
        *state,
        hop_own,
        hop_pair,
    )
    peers = grad.reshape(hn, groups * count, lines, feats).transpose(1, 0, 2, 3)
    got = lax.all_to_all(peers.astype(WIRE), ("grp", "seq"), 0, 0, tiled=True)
    parts = got.reshape(groups, chips, 2, hn, lines, feats).astype(F32)
    return parts.sum(1).transpose(1, 0, 2, 3, 4).reshape(queries.shape[0], lines, feats)


def solution(mesh):
    return jax.shard_map(
        per_device,
        mesh=mesh,
        in_specs=(
            P("head", "seq", None),
            P("head", "seq", None),
            P("head", "seq", None),
            P("head", None, None),
        ),
        out_specs=P("head", ("grp", "seq"), None),
        check_vma=False,
    )
```

time: 39.1 us -> 21.6 us (0.55)
  Pallas kernels: 18 us -> 3.71 us
  blocking collectives: 0 us -> 10.5 us
  waiting for transfers between devices: 6.69 us -> 0.89 us
  starting transfers between devices: 8.12 us -> 3.63 us
  local copies, waits for them, and re-layouts: 4.6 us -> 2.51 us
  other arithmetic: 1.3 us -> 0.11 us
    pallas_call x1 -> x2, Pallas kernels: 18 us -> 3.71 us  [call(): pl.pallas_call(function, in_specs=[pl.BlockSpec(memory_space=pltpu.SMEM)]...]
    all_to_all x0 -> x1, blocking collectives: none -> 10.5 us  [per_device(): got = lax.all_to_all(peers.astype(WIRE), ('grp', 'seq'), 0, 0, tiled=True)]
    ppermute x4 -> x2, waiting for transfers between devices: 6.03 us -> 0.88 us  [the longest x1 0.58 us: per_device(): hops.append(lax.ppermute(kv, 'seq', ring))]
    ppermute x4 -> x2, starting transfers between devices: 8.04 us -> 3.63 us  [the longest x1 3.05 us: per_device(): hops.append(lax.ppermute(kv, 'seq', ring))]
    dynamic_slice x4 -> x0, local copies, waits for them, and re-layouts: 1.75 us -> none  [the longest x1 0.97 us: per_device(): grad = lax.dynamic_slice_in_dim(grad, lax.axis_index('grp') * mine, mine, 1)]
    squeeze x1 -> x2, local copies, waits for them, and re-layouts: 1.85 us -> 1 us  [mine(): return lax.dynamic_index_in_dim(split_heads, half * groups + grp, 0, False)]
    add x1 -> x0, other arithmetic: 0.67 us -> none  [per_device(): result = result + lax.ppermute(send, 'seq', ring)]
    transpose x0 -> x1, local copies, waits for them, and re-layouts: none -> 0.66 us  [per_device(): parts.sum(1).transpose(1, 0, 2, 3, 4)]
  transfers between devices with their start and end apart: 6 -> 4, of which waited for: 4 -> 2; matrix products, arithmetic and copies ran while one was open for 3% -> 5% of each run, Pallas kernels for 0% -> 7%
where the time goes in v2:
time: 21.6 us; the launch traced here: 21.4 us
  blocking collectives  10.5 us (49%)
  Pallas kernels  3.71 us (17%)
  starting transfers between devices  3.63 us (17%)
  local copies, waits for them, and re-layouts  2.51 us (12%)
  waiting for transfers between devices  0.89 us (4%)
    all_to_all x1, blocking collectives, per_device(): got = lax.all_to_all(peers.astype(WIRE), ('grp', 'seq'), 0, 0, tiled=True)  10.5 us
    pallas_call x2, Pallas kernels, call(): pl.pallas_call(function, in_specs=[pl.BlockSpec(memory_space=pltpu.SMEM)]...  3.71 us
    ppermute x1, starting transfers between devices, per_device(): hops.append(lax.ppermute(kv, 'seq', ring))  3.05 us
    squeeze x2, local copies, waits for them, and re-layouts, mine(): return lax.dynamic_index_in_dim(split_heads, half * groups + grp, 0, False)  1 us
    unnamed x5, local copies, waits for them, and re-layouts  0.84 us
    transpose x1, local copies, waits for them, and re-layouts, per_device(): parts.sum(1).transpose(1, 0, 2, 3, 4)  0.66 us
    ppermute x1, waiting for transfers between devices, per_device(): hops.append(lax.ppermute(kv, 'seq', ring))  0.58 us
    ppermute x1, starting transfers between devices, per_device(): q_pair = lax.ppermute(mine(queries, 1 - core), 'seq', swap)  0.57 us
  transfers between devices with their start and end apart: 4, of which 2 were waited for; matrix products, arithmetic and copies ran while one was open for 5% of the time, Pallas kernels for 7%

profile of v2, /device:TPU:0, one launch (start us, length us, event | category | flops | bytes accessed | tf_op | source)
XLA Modules:
  0.0 21.4 jit_solution(8378551764867363320)
XLA Ops:
  0.0 0.0 copy-start
  0.0 0.0 copy-start.1
  0.0 0.8 %constant_dynamic-update-slice_fusion.1 = bf16[2,128,128]{2,1,0:T(8,128)(2,1)S(1)} fusion(bf16[1,128,128]{2,1,0:T(8,128)(2,1)} %param.5), kind=kLoop, calls=%fused_computation.6 | loop fusion | bytes 65536
  0.8 0.0 copy-done.1
  0.8 3.1 %collective-permute-start.2 = (bf16[2,128,128]{2,1,0:T(8,128)(2,1)S(1)}, bf16[2,128,128]{2,1,0:T(8,128)(2,1)S(1)}, u32[]{:S(2)}, u32[]{:S(2)}) collective-permute-start(bf16[2,128,128]{2,1,0:T(8,128)(2,1)S(1)} %constant_dynamic-update-slice_fusion.r_4_), channel_id=1, source_target_pairs={{0,2},{1,3},{2,0},{3,1},{4,6},{5,7},{6,4},{7,5},{8,10},{9,11},{10,... | collective-permute-start | bytes 196616 | tf_op jit(solution)/shard_map/ppermute | solution.py:223
  3.9 0.0 collective-permute-start.1
  3.9 1.0 %dynamic-slice_bitcast_fusion.1 = (bf16[4,128,128]{2,1,0:T(8,128)(2,1)S(1)}, bf16[4,128,128]{2,1,0:T(8,128)(2,1)S(1)}) fusion(bf16[4,4,128,128]{3,2,1,0:T(8,128)(2,1)} %bitcast.27, s32[]{:T(128)S(6)} %select_n.9, s32[]{:T(128)S(6)} %select_n.8), kind=kLoop, calls=%fused_computation.3 | loop fusion | bytes 524296 | tf_op jit(solution)/shard_map/jit(dynamic_index_in_dim)/squeeze | solution.py:217
  4.9 0.6 %collective-permute-start = (bf16[4,128,128]{2,1,0:T(8,128)(2,1)S(1)}, bf16[4,128,128]{2,1,0:T(8,128)(2,1)S(1)}, u32[]{:S(2)}, u32[]{:S(2)}) collective-permute-start(bf16[4,128,128]{2,1,0:T(8,128)(2,1)S(1)} %get-tuple-element.11), channel_id=1, source_target_pairs={{0,1},{1,0},{2,3},{3,2},{4,5},{5,4},{6,7},{7,6},{8,9},{9,8},{10,11... | collective-permute-start | bytes 393224 | tf_op jit(solution)/shard_map/ppermute | solution.py:226
  5.5 0.0 copy-done
  5.5 0.1 pad_add_fusion.r_0_
  5.6 0.6 %collective-permute-done.2 = bf16[2,128,128]{2,1,0:T(8,128)(2,1)S(1)} collective-permute-done((bf16[2,128,128]{2,1,0:T(8,128)(2,1)S(1)}, bf16[2,128,128]{2,1,0:T(8,128)(2,1)S(1)}, u32[]{:S(2)}, u32[]{:S(2)}) %collective-permute-start.2) | collective-permute-done | bytes 65568 | tf_op jit(solution)/shard_map/ppermute | solution.py:223
  6.1 0.0 collective-permute-start.3
  6.1 0.0 collective-permute-done.1.r_5_
  6.2 0.3 %collective-permute-done.r_2_ = bf16[4,128,128]{2,1,0:T(8,128)(2,1)S(1)} collective-permute-done((bf16[4,128,128]{2,1,0:T(8,128)(2,1)S(1)}, bf16[4,128,128]{2,1,0:T(8,128)(2,1)S(1)}, u32[]{:S(2)}, u32[]{:S(2)}) %collective-permute-start) | collective-permute-done | bytes 131104 | tf_op jit(solution)/shard_map/ppermute | solution.py:226
  6.5 1.6 %shard_map.46 = (f32[4,256,128]{2,1,0:T(8,128)S(1)}, f32[4,256,1]{2,1,0:T(8,128)S(1)}, f32[4,256,256]{2,1,0:T(8,128)S(1)}) custom-call(s32[2]{0:T(128)S(1)} %pad_add_fusion.r_0_, bf16[4,128,128]{2,1,0:T(8,128)(2,1)S(1)} %get-tuple-element.12.r_1_, bf16[4,128,128]{2,1,0:T(8,128)(2,1)S(1)} %collective-permute-done.r_2_, ...), custom_call_target="tpu_custom_call" | custom-call | flops 2000000000 | bytes 10000000 | tf_op jit(solution)/shard_map/pallas_call | solution.py:192
  8.1 0.0 collective-permute-done.3.r_10_
  8.1 2.1 %shard_map.47 = f32[4,128,128]{2,1,0:T(8,128)S(1)} custom-call(s32[2]{0:T(128)S(1)} %pad_add_fusion.r_0_, bf16[4,128,128]{2,1,0:T(8,128)(2,1)S(1)} %get-tuple-element.12.r_1_, bf16[4,128,128]{2,1,0:T(8,128)(2,1)S(1)} %collective-permute-done.r_2_, bf16[4,128,128]{2,1,0:T(8,128)(2,1)S(1)} %dynamic-slice_bitcast_fusion.r_3_, ...), custom_call_target="tpu_custom_call" | custom-call | flops 2000000000 | bytes 10000000 | tf_op jit(solution)/shard_map/pallas_call | solution.py:192
  10.2 10.5 %all_to_all.5 = bf16[8,4,16,128]{3,2,1,0:T(8,128)(2,1)S(1)} all-to-all(bf16[8,4,16,128]{3,2,1,0:T(8,128)(2,1)S(1)} %bitcast.24), channel_id=1, replica_groups=mesh['grp'=2,'head'=4,'seq'=4] {'grp','seq'}, dimensions={0} | all-to-all | bytes 262144 | tf_op jit(solution)/shard_map/all_to_all | solution.py:242
  20.7 0.7 %copy.9 = f32[2,2,4,16,128]{4,3,2,1,0:T(8,128)} copy(f32[2,2,4,16,128]{4,3,2,0,1:T(8,128)S(1)} %bitcast.26) | data formatting | bytes 262144 | tf_op jit(solution)/shard_map/transpose | solution.py:244
  (5 shorter events, 0.1 us)
Async XLA Ops:
  0.0 5.5 %copy-start = (bf16[16,128,128]{2,1,0:T(8,128)(2,1)S(1)}, bf16[16,128,128]{2,1,0:T(8,128)(2,1)}, u32[]{:S(2)}) copy-start(bf16[16,128,128]{2,1,0:T(8,128)(2,1)} %param.7) | copy-start | bytes 1572868
  0.0 0.8 %copy-start.1 = (bf16[1,128,128]{2,1,0:T(8,128)(2,1)S(1)}, bf16[1,128,128]{2,1,0:T(8,128)(2,1)}, u32[]{:S(2)}) copy-start(bf16[1,128,128]{2,1,0:T(8,128)(2,1)} %param.6) | copy-start | bytes 98308
  0.8 5.3 %collective-permute-start.2 = (bf16[2,128,128]{2,1,0:T(8,128)(2,1)S(1)}, bf16[2,128,128]{2,1,0:T(8,128)(2,1)S(1)}, u32[]{:S(2)}, u32[]{:S(2)}) collective-permute-start(bf16[2,128,128]{2,1,0:T(8,128)(2,1)S(1)} %constant_dynamic-update-slice_fusion.r_4_), channel_id=1, source_target_pairs={{0,2},{1,3},{2,0},{3,1},{4,6},{5,7},{6,4},{7,5},{8,10},{9,11},{10,... | collective-permute-start | bytes 196616 | tf_op jit(solution)/shard_map/ppermute | solution.py:223
  3.9 2.3 %collective-permute-start.1 = (bf16[2,128,128]{2,1,0:T(8,128)(2,1)S(1)}, bf16[2,128,128]{2,1,0:T(8,128)(2,1)S(1)}, u32[]{:S(2)}, u32[]{:S(2)}) collective-permute-start(bf16[2,128,128]{2,1,0:T(8,128)(2,1)S(1)} %constant_dynamic-update-slice_fusion.r_4_), channel_id=1, source_target_pairs={{0,1},{1,0},{2,3},{3,2},{4,5},{5,4},{6,7},{7,6},{8,9},{9,8},{10,11... | collective-permute-start | bytes 196616 | tf_op jit(solution)/shard_map/ppermute | solution.py:225
  4.9 1.6 %collective-permute-start = (bf16[4,128,128]{2,1,0:T(8,128)(2,1)S(1)}, bf16[4,128,128]{2,1,0:T(8,128)(2,1)S(1)}, u32[]{:S(2)}, u32[]{:S(2)}) collective-permute-start(bf16[4,128,128]{2,1,0:T(8,128)(2,1)S(1)} %get-tuple-element.11), channel_id=1, source_target_pairs={{0,1},{1,0},{2,3},{3,2},{4,5},{5,4},{6,7},{7,6},{8,9},{9,8},{10,11... | collective-permute-start | bytes 393224 | tf_op jit(solution)/shard_map/ppermute | solution.py:226
  6.1 1.9 %collective-permute-start.3 = (bf16[1,2,128,128]{3,2,1,0:T(8,128)(2,1)S(1)}, bf16[1,2,128,128]{3,2,1,0:T(8,128)(2,1)S(1)}, u32[]{:S(2)}, u32[]{:S(2)}) collective-permute-start(bf16[1,2,128,128]{3,2,1,0:T(8,128)(2,1)S(1)} %bitcast.21), channel_id=1, source_target_pairs={{0,1},{1,0},{2,3},{3,2},{4,5},{5,4},{6,7},{7,6},{8,9},{9,8},{10,11... | collective-permute-start | bytes 196616 | tf_op jit(solution)/shard_map/ppermute | solution.py:232

commit v3 on v2

v3 whole, which is shorter than its diff:
```python
import jax
import jax.numpy as jnp
from jax import lax
from jax.experimental import pallas as pl
from jax.experimental.pallas import tpu as pltpu
from jax.sharding import PartitionSpec as P

F32 = jnp.float32
BF16 = jnp.bfloat16
WIRE = BF16
NN = (((1,), (0,)), ((), ()))
NT = (((1,), (1,)), ((), ()))
TN = (((0,), (0,)), ((), ()))


def mm(a, b, dims=NN):
    return lax.dot_general(a, b, dims, preferred_element_type=F32)


def split(x):
    high = x.astype(BF16)
    return high, (x - high.astype(F32)).astype(BF16)


def cat(parts, axis):
    return jnp.concatenate(parts, axis)


def interleave(make, heads, step):
    def group(i, _):
        running = [make(i * step + j) for j in range(step)]
        while running:
            running = [r for r in running if next(r, True) is None]
        return 0

    lax.fori_loop(0, heads // step, group, 0)


def add_rows(x):
    return jnp.sum(x, axis=0, keepdims=True)


def own_block(core, kv_own, kv_pair):
    tokens = kv_own.shape[1]
    rows = 2 * tokens

    def position(axis):
        index = lax.broadcasted_iota(jnp.int32, (rows, rows), axis)
        return jnp.where((index < tokens) == (core == 0), index % tokens, tokens + index % tokens)

    key = cat([kv_own[0], kv_pair[0]], 0)
    value = cat([kv_own[1], kv_pair[1]], 0)
    return position(0) <= position(1), key, value


def features(wmat_t, query, key):
    return jnp.exp(mm(wmat_t, query, NT)), jnp.exp(mm(wmat_t, key, NT))


def first_body(step, place, q_own, q_pair, w_ref, kv_own, kv_pair, state_ref):
    dh = q_own.shape[-1]
    scale = 1.0 / (dh**0.5)
    seen, key, value = own_block(place[0], kv_own, kv_pair)
    value_t = value.T
    heads, _, _ = w_ref.shape

    def forward(h):
        query = cat([q_own[h], q_pair[h]], 0)
        wmat_t = w_ref[h].T
        phi_q, phi_k = features(wmat_t, query, key)
        yield
        p = jnp.where(seen, jnp.exp(mm(key, query, NT) * scale), 0.0)
        yield
        a = jnp.where(seen, mm(phi_k.astype(BF16), phi_q.astype(BF16), TN), 0.0)
        yield
        sums = cat([add_rows(p), add_rows(a), jnp.zeros((6, p.shape[1]), F32)], 0)
        state_ref[h, 2 * dh :] = sums
        state_ref[h, :dh] = mm(value_t, p.astype(BF16))
        yield
        state_ref[h, dh : 2 * dh] = mm(cat([value_t, value_t], 1), cat(split(a), 0))

    interleave(forward, heads, step)


def second_body(total, step, place, q_own, q_pair, w_ref, kv_own, kv_pair, state_ref, hop_own, hop_pair, grad_ref):
    dh = q_own.shape[-1]
    core, chip = place[0], place[1]
    scale = 1.0 / (dh**0.5)
    hops = hop_own.shape[0]
    heads, _, feats = w_ref.shape

    def hop_block(hop):
        key_j = cat([hop_own[hop, 0], hop_pair[hop, 0]], 0)
        return key_j, cat([hop_own[hop, 1], hop_pair[hop, 1]], 0)

    def cotangents(numer_t, denom_t, numer_s, denom_s):
        target = (numer_t * (1.0 / denom_t)).astype(BF16).astype(F32)
        inverse = 1.0 / denom_s
        student = numer_s * inverse
        g = ((student - target) * (inverse * (2.0 / total))).astype(BF16)
        return g, add_rows(g.astype(F32) * student)

    def score_back(seen, value, g, shift):
        return split(jnp.where(seen, mm(value, g) - shift, 0.0))

    def local_back(dah, dal, qh, kh):
        dphi_q = mm(cat([kh, kh], 1), cat([dah, dal], 0))
        return dphi_q, mm(cat([qh, qh], 1), cat([dah, dal], 1), NT)

    def stacked(dz):
        return cat(split(dz), 0)

    def saved(h):
        numer_t, numer_s = state_ref[h, :dh], state_ref[h, dh : 2 * dh]
        sums = state_ref[h, 2 * dh :]
        return numer_t, sums[0:1], numer_s, sums[1:2]

    def finish(h, wide):
        grad_ref[h] = (wide[:feats] + wide[feats:]).T

    def whole(h):
        seen, key, value = own_block(core, kv_own, kv_pair)
        query = cat([q_own[h], q_pair[h]], 0)
        wmat_t = w_ref[h].T

        def earlier(hop, carry):
            state, state_t, total_j, numer_t, denom_t = carry[:5]
            key_j, value_j = hop_block(hop)
            if pre is None:
                p = jnp.exp(mm(key_j, query, NT) * scale)
                phi_j = jnp.exp(mm(wmat_t, key_j, NT))
            else:
                p, phi_j = pre
            ph = phi_j.astype(BF16)
            value_jt = value_j.T
            denom_t = denom_t + add_rows(p)
            numer_t = numer_t + mm(value_jt, p.astype(BF16))
            state = state + mm(ph, value_j)
            state_t = state_t + mm(value_jt, ph, NT)
            total_j = total_j + jnp.sum(ph.astype(F32), axis=1, keepdims=True)
            sums = (state, state_t, total_j, numer_t, denom_t)
            return sums + (phi_j,) if hops == 1 else sums

        numer_t, denom_t, numer_s, denom_s = saved(h)
        phi_q, phi_k = features(wmat_t, query, key)
        qh, kh = phi_q.astype(BF16), phi_k.astype(BF16)
        square = jnp.zeros((feats, dh), F32), jnp.zeros((dh, feats), F32)
        carry = square + (jnp.zeros((feats, 1), F32), numer_t, denom_t)
        pre = None
        if hops == 1:
            key_j = hop_block(0)[0]
            phi_j = jnp.exp(mm(wmat_t, key_j, NT))
            yield
            pre = jnp.exp(mm(key_j, query, NT) * scale), phi_j
            yield
            carry = earlier(0, carry)
        else:
            carry = lax.fori_loop(0, chip, earlier, carry)
        state, state_t, total_j, numer_t, denom_t = carry[:5]
        yield
        numer_s = numer_s + mm(cat(split(state_t), 1), cat([qh, qh], 0))
        denom_s = denom_s + add_rows(qh.astype(F32) * total_j)
        yield
        g, shift = cotangents(numer_t, denom_t, numer_s, denom_s)
        yield
        dah, dal = score_back(seen, value, g, shift)
        ds = mm(qh, g, NT)
        yield
        dphi_q, dphi_k = local_back(dah, dal, qh, kh)
        yield
        lost = jnp.sum(qh.astype(F32) * shift, axis=1, keepdims=True)
        dphi_q = dphi_q + mm(cat(split(state), 1), cat([g, g], 0)) - total_j * shift
        yield
        dsw = cat(split(ds), 1)

        def step_back(value_j, phi_j):
            return stacked((mm(dsw, cat([value_j, value_j], 1), NT) - lost) * phi_j)

        if hops == 1:
            key_j, value_j = hop_block(0)
            dz_j = step_back(value_j, carry[5])
            yield
            dz_q = stacked(dphi_q * phi_q)
            dz_k = stacked(dphi_k * phi_k)
            yield
            wide = mm(cat([dz_q, dz_k, dz_j], 1), cat([query, key, key_j], 0))
        else:
            dz = cat([stacked(dphi_q * phi_q), stacked(dphi_k * phi_k)], 1)
            wide = mm(dz, cat([query, key], 0))

            def back(hop, wide):
                key_j, value_j = hop_block(hop)
                phi_j = jnp.exp(mm(wmat_t, key_j, NT))
                return wide + mm(step_back(value_j, phi_j), key_j)

            wide = lax.fori_loop(0, chip, back, wide)
        yield
        finish(h, wide)

    @pl.when(chip != 0)
    def _():
        interleave(whole, heads, step)

    def alone(h):
        seen, key, value = own_block(core, kv_own, kv_pair)
        query = cat([q_own[h], q_pair[h]], 0)
        wmat_t = w_ref[h].T
        numer_t, denom_t, numer_s, denom_s = saved(h)
        phi_q, phi_k = features(wmat_t, query, key)
        qh, kh = phi_q.astype(BF16), phi_k.astype(BF16)
        g, shift = cotangents(numer_t, denom_t, numer_s, denom_s)
        yield
        dah, dal = score_back(seen, value, g, shift)
        yield
        dphi_q, dphi_k = local_back(dah, dal, qh, kh)
        yield
        dz = cat([stacked(dphi_q * phi_q), stacked(dphi_k * phi_k)], 1)
        wide = mm(dz, cat([query, key], 0))
        yield
        finish(h, wide)

    @pl.when(chip == 0)
    def _():
        interleave(alone, heads, step)


def call(function, outs, *operands):
    vmem = pl.BlockSpec(memory_space=pltpu.VMEM)
    return pl.pallas_call(
        function,
        in_specs=[pl.BlockSpec(memory_space=pltpu.SMEM)] + [vmem] * (len(operands) - 1),
        out_specs=[vmem] * len(outs),
        out_shape=[jax.ShapeDtypeStruct(s, F32) for s in outs],
        compiler_params=pltpu.CompilerParams(vmem_limit_bytes=16 << 20),
        cost_estimate=pl.CostEstimate(flops=2 * 10**9, bytes_accessed=10**7, transcendentals=10**6),
    )(*operands)


def per_device(queries, keys, values, feature_map):
    count, groups = lax.axis_size("seq"), lax.axis_size("grp")
    chips = count // 2
    seq, grp = lax.axis_index("seq"), lax.axis_index("grp")
    core, chip = seq & 1, seq >> 1
    tokens, dh = keys.shape[1:]
    total = tokens * count
    feats = feature_map.shape[2]
    hn = queries.shape[0] // (2 * groups)
    lines = dh // (groups * count)
    step = hn if hn <= 4 else 1
    swap = [(i, i ^ 1) for i in range(count)]

    def mine(array, half):
        split_heads = array.reshape(2 * groups, hn, *array.shape[1:])
        return lax.dynamic_index_in_dim(split_heads, half * groups + grp, 0, False)

    kv = jnp.where(lax.broadcasted_iota(jnp.int32, (2, tokens, dh), 0) == 0, keys, values)
    hops = []
    for k in range(1, chips):
        ring = [(i, (i + 2 * k) % count) for i in range(count)]
        hops.append(lax.ppermute(kv, "seq", ring))
    place = jnp.stack([core, chip]).astype(jnp.int32)
    kv_pair = lax.ppermute(kv, "seq", swap)
    q_pair = lax.ppermute(mine(queries, 1 - core), "seq", swap)
    local = (place, mine(queries, core), q_pair, mine(feature_map, core), kv, kv_pair)
    rows = 2 * tokens
    state = [(hn, 2 * dh + 8, rows)]
    state = call(lambda *r: first_body(step, *r), state, *local)
    hop_own = jnp.stack(hops)
    hop_pair = lax.ppermute(hop_own, "seq", swap)
    (grad,) = call(
        lambda *r: second_body(total, step, *r),
        [(hn, dh, feats)],
        *local,
        *state,
        hop_own,
        hop_pair,
    )
    grad = grad.reshape(hn, groups, chips, 2, lines, feats)
    keep = lax.dynamic_index_in_dim(grad, core, 3, False)
    got = lax.ppermute(lax.dynamic_index_in_dim(grad, 1 - core, 3, False), "seq", swap)
    low = core == 0
    part = jnp.stack([jnp.where(low, keep, got), jnp.where(low, got, keep)])

    def rows_for(turn, ahead):
        there = lax.dynamic_index_in_dim(part, (grp + turn) % groups, 2, False)
        return lax.dynamic_index_in_dim(there, (chip + ahead) % chips, 2, False)

    received = [rows_for(0, 0)] + [0.0] * (groups - 1)
    for turn, ahead in sends(groups, chips):
        route = [
            (g * count + 2 * y + c, (g + turn) % groups * count + 2 * ((y + ahead) % chips) + c)
            for g in range(groups)
            for y in range(chips)
            for c in range(2)
        ]
        sent = lax.ppermute(rows_for(turn, ahead).astype(WIRE), ("grp", "seq"), route)
        received[turn] = received[turn] + sent.astype(F32)
    slots = []
    for slot in range(groups):
        piece = received[0]
        for turn in range(1, groups):
            piece = jnp.where((grp - slot) % groups == turn, received[turn], piece)
        slots.append(piece)
    return jnp.stack(slots, 1).reshape(queries.shape[0], lines, feats)


def sends(groups, chips):
    across = [(turn, ahead) for ahead in range(1, chips) for turn in reversed(range(groups))]
    beside = [(turn, 0) for turn in range(1, groups)]
    return beside + across


def solution(mesh):
    return jax.shard_map(
        per_device,
        mesh=mesh,
        in_specs=(
            P("head", "seq", None),
            P("head", "seq", None),
            P("head", "seq", None),
            P("head", None, None),
        ),
        out_specs=P("head", ("grp", "seq"), None),
        check_vma=False,
    )
```

time: 21.6 us -> 21.1 us (0.977)
  blocking collectives: 10.5 us -> 0 us
  waiting for transfers between devices: 0.89 us -> 6.26 us
  starting transfers between devices: 3.63 us -> 8.3 us
  other arithmetic: 0.11 us -> 1.07 us
  local copies, waits for them, and re-layouts: 2.51 us -> 1.68 us
    all_to_all x1 -> x0, blocking collectives: 10.5 us -> none  [per_device(): got = lax.all_to_all(peers.astype(WIRE), ('grp', 'seq'), 0, 0, tiled=True)]
    ppermute x0 -> x4, starting transfers between devices: none -> 4.96 us  [the longest x3 4.39 us: per_device(): lax.ppermute(rows_for(turn, ahead).astype(WIRE), ('grp', 'seq'), route)]
    ppermute x0 -> x4, waiting for transfers between devices: none -> 4.87 us  [the longest x3 3.88 us: per_device(): lax.ppermute(rows_for(turn, ahead).astype(WIRE), ('grp', 'seq'), route)]
    select_n x0 -> x1, other arithmetic: none -> 0.91 us  [per_device(): jnp.where(lax.broadcasted_iota(jnp.int32, (2, tokens, dh), 0) == 0, keys,...]
    unnamed x5 -> x2, local copies, waits for them, and re-layouts: 0.84 us -> 0.01 us
    ppermute x1, waiting for transfers between devices: 0.58 us -> 1.38 us  [per_device(): hops.append(lax.ppermute(kv, 'seq', ring))]
    another operation x0 -> x1, local copies, waits for them, and re-layouts: none -> 0.66 us  [per_device(): return jnp.stack(slots, 1).reshape(queries.shape[0], lines, feats)]
    transpose x1 -> x0, local copies, waits for them, and re-layouts: 0.66 us -> none  [per_device(): parts.sum(1).transpose(1, 0, 2, 3, 4)]
  transfers between devices with their start and end apart: 4 -> 8, of which waited for: 2 -> 4; matrix products, arithmetic and copies ran while one was open for 5% -> 5% of each run, Pallas kernels for 7% -> 8%
where the time goes in v3:
time: 21.1 us; the launch traced here: 21 us
  starting transfers between devices  8.3 us (39%)
  waiting for transfers between devices  6.26 us (30%)
  Pallas kernels  3.57 us (17%)
  local copies, waits for them, and re-layouts  1.68 us (8%)
  other arithmetic  1.07 us (5%)
    ppermute x3, starting transfers between devices, per_device(): lax.ppermute(rows_for(turn, ahead).astype(WIRE), ('grp', 'seq'), route)  4.39 us
    ppermute x3, waiting for transfers between devices, per_device(): lax.ppermute(rows_for(turn, ahead).astype(WIRE), ('grp', 'seq'), route)  3.88 us
    pallas_call x2, Pallas kernels, call(): pl.pallas_call(function, in_specs=[pl.BlockSpec(memory_space=pltpu.SMEM)]...  3.57 us
    ppermute x1, starting transfers between devices, per_device(): hops.append(lax.ppermute(kv, 'seq', ring))  2.58 us
    ppermute x1, waiting for transfers between devices, per_device(): hops.append(lax.ppermute(kv, 'seq', ring))  1.38 us
    squeeze x2, local copies, waits for them, and re-layouts, mine(): return lax.dynamic_index_in_dim(split_heads, half * groups + grp, 0, False)  0.99 us
    ppermute x1, waiting for transfers between devices, per_device(): lax.ppermute(lax.dynamic_index_in_dim(grad, 1 - core, 3, False), 'seq', s...  0.99 us
    select_n x1, other arithmetic, per_device(): jnp.where(lax.broadcasted_iota(jnp.int32, (2, tokens, dh), 0) == 0, keys,...  0.91 us
  transfers between devices with their start and end apart: 8, of which 4 were waited for; matrix products, arithmetic and copies ran while one was open for 5% of the time, Pallas kernels for 8%

profile of v3, /device:TPU:0, one launch (start us, length us, event | category | flops | bytes accessed | tf_op | source)
XLA Modules:
  0.0 21.0 jit_solution(1814828349041982867)
XLA Ops:
  0.0 0.0 copy-start
  0.0 0.9 %broadcast_select_fusion.r_4_ = bf16[2,128,128]{2,1,0:T(8,128)(2,1)S(1)} fusion(pred[2]{0:T(512)(128)(4,1)S(1)} %iota_compare_fusion, bf16[128,128]{1,0:T(8,128)(2,1)} %bitcast.68, bf16[128,128]{1,0:T(8,128)(2,1)} %bitcast.69), kind=kLoop, calls=%fused_computation.31 | loop fusion | flops 32768 | bytes 131074 | tf_op jit(solution)/shard_map/jit(_where)/select_n | solution.py:256
  0.9 0.5 %collective-permute-start.1 = (bf16[2,128,128]{2,1,0:T(8,128)(2,1)S(1)}, bf16[2,128,128]{2,1,0:T(8,128)(2,1)S(1)}, u32[]{:S(2)}, u32[]{:S(2)}) collective-permute-start(bf16[2,128,128]{2,1,0:T(8,128)(2,1)S(1)} %broadcast_select_fusion.r_4_), channel_id=1, source_target_pairs={{0,1},{1,0},{2,3},{3,2},{4,5},{5,4},{6,7},{7,6},{8,9},{9,8},{10,11... | collective-permute-start | bytes 196616 | tf_op jit(solution)/shard_map/ppermute | solution.py:262
  1.5 2.6 %collective-permute-start.2 = (bf16[2,128,128]{2,1,0:T(8,128)(2,1)S(1)}, bf16[2,128,128]{2,1,0:T(8,128)(2,1)S(1)}, u32[]{:S(2)}, u32[]{:S(2)}) collective-permute-start(bf16[2,128,128]{2,1,0:T(8,128)(2,1)S(1)} %broadcast_select_fusion.r_4_), channel_id=1, source_target_pairs={{0,2},{1,3},{2,0},{3,1},{4,6},{5,7},{6,4},{7,5},{8,10},{9,11},{10,... | collective-permute-start | bytes 196616 | tf_op jit(solution)/shard_map/ppermute | solution.py:260
  4.0 1.0 %dynamic-slice_bitcast_fusion.2 = (bf16[4,128,128]{2,1,0:T(8,128)(2,1)S(1)}, bf16[4,128,128]{2,1,0:T(8,128)(2,1)S(1)}) fusion(bf16[4,4,128,128]{3,2,1,0:T(8,128)(2,1)} %bitcast.67, s32[]{:T(128)S(6)} %select_n.108, s32[]{:T(128)S(6)} %select_n.107), kind=kLoop, calls=%fused_computation.15 | loop fusion | bytes 524296 | tf_op jit(solution)/shard_map/jit(dynamic_index_in_dim)/squeeze | solution.py:254
  5.0 0.2 %collective-permute-start = (bf16[4,128,128]{2,1,0:T(8,128)(2,1)S(1)}, bf16[4,128,128]{2,1,0:T(8,128)(2,1)S(1)}, u32[]{:S(2)}, u32[]{:S(2)}) collective-permute-start(bf16[4,128,128]{2,1,0:T(8,128)(2,1)S(1)} %get-tuple-element.5), channel_id=1, source_target_pairs={{0,1},{1,0},{2,3},{3,2},{4,5},{5,4},{6,7},{7,6},{8,9},{9,8},{10,11... | collective-permute-start | bytes 393224 | tf_op jit(solution)/shard_map/ppermute | solution.py:263
  5.2 0.0 copy-done
  5.3 0.1 pad_add_fusion.r_0_
  5.3 1.4 %collective-permute-done.2 = bf16[2,128,128]{2,1,0:T(8,128)(2,1)S(1)} collective-permute-done((bf16[2,128,128]{2,1,0:T(8,128)(2,1)S(1)}, bf16[2,128,128]{2,1,0:T(8,128)(2,1)S(1)}, u32[]{:S(2)}, u32[]{:S(2)}) %collective-permute-start.2) | collective-permute-done | bytes 65568 | tf_op jit(solution)/shard_map/ppermute | solution.py:260
  6.7 0.0 collective-permute-start.3
  6.7 0.0 collective-permute-done.1.r_5_
  6.7 0.0 collective-permute-done.r_2_
  6.7 1.6 %shard_map.46.r_6_ = f32[4,264,256]{2,1,0:T(8,128)S(1)} custom-call(s32[2]{0:T(128)S(1)} %pad_add_fusion.r_0_, bf16[4,128,128]{2,1,0:T(8,128)(2,1)S(1)} %get-tuple-element.6.r_1_, bf16[4,128,128]{2,1,0:T(8,128)(2,1)S(1)} %collective-permute-done.r_2_, bf16[4,128,128]{2,1,0:T(8,128)(2,1)S(1)} %dynamic-slice_bitcast_fusion.1.r_3_, ...), custom_call_target="tpu_custom_call" | custom-call | flops 2000000000 | bytes 10000000 | tf_op jit(solution)/shard_map/pallas_call | solution.py:229
  8.4 0.0 collective-permute-done.3.r_8_
  8.4 2.0 %shard_map.47 = f32[4,128,128]{2,1,0:T(8,128)S(1)} custom-call(s32[2]{0:T(128)S(1)} %pad_add_fusion.r_0_, bf16[4,128,128]{2,1,0:T(8,128)(2,1)S(1)} %get-tuple-element.6.r_1_, bf16[4,128,128]{2,1,0:T(8,128)(2,1)S(1)} %collective-permute-done.r_2_, bf16[4,128,128]{2,1,0:T(8,128)(2,1)S(1)} %dynamic-slice_bitcast_fusion.1.r_3_, ...), custom_call_target="tpu_custom_call" | custom-call | flops 2000000000 | bytes 10000000 | tf_op jit(solution)/shard_map/pallas_call | solution.py:229
  10.4 0.6 %collective-permute-start.4 = (f32[4,2,2,16,128]{4,3,2,1,0:T(8,128)S(1)}, f32[4,2,2,16,128]{4,3,2,1,0:T(8,128)S(1)}, u32[]{:S(2)}, u32[]{:S(2)}) collective-permute-start(f32[4,2,2,16,128]{4,3,2,1,0:T(8,128)S(1)} %dynamic-slice_bitcast_fusion), channel_id=1, source_target_pairs={{0,1},{1,0},{2,3},{3,2},{4,5},{5,4},{6,7},{7,6},{8,9},{9,8},{10,11... | collective-permute-start | bytes 393224 | tf_op jit(solution)/shard_map/ppermute | solution.py:280
  10.9 1.0 %collective-permute-done.4 = f32[4,2,2,16,128]{4,3,2,1,0:T(8,128)S(1)} collective-permute-done((f32[4,2,2,16,128]{4,3,2,1,0:T(8,128)S(1)}, f32[4,2,2,16,128]{4,3,2,1,0:T(8,128)S(1)}, u32[]{:S(2)}, u32[]{:S(2)}) %collective-permute-start.4) | collective-permute-done | bytes 131104 | tf_op jit(solution)/shard_map/ppermute | solution.py:280
  12.0 1.8 %collective-permute-start.5 = (bf16[2,4,16,128]{3,2,1,0:T(8,128)(2,1)S(1)}, bf16[2,4,16,128]{3,2,1,0:T(8,128)(2,1)S(1)}, u32[]{:S(2)}, u32[]{:S(2)}) collective-permute-start(bf16[2,4,16,128]{3,2,1,0:T(8,128)(2,1)S(1)} %get-tuple-element.12), channel_id=1, source_target_pairs={{0,16},{1,17},{2,18},{3,19},{16,0},{17,1},{18,2},{19,3},{4,20},{5,... | collective-permute-start | bytes 98312 | tf_op jit(solution)/shard_map/ppermute | solution.py:296
  13.8 2.6 %collective-permute-start.6 = (bf16[2,4,16,128]{3,2,1,0:T(8,128)(2,1)S(1)}, bf16[2,4,16,128]{3,2,1,0:T(8,128)(2,1)S(1)}, u32[]{:S(2)}, u32[]{:S(2)}) collective-permute-start(bf16[2,4,16,128]{3,2,1,0:T(8,128)(2,1)S(1)} %get-tuple-element.13), channel_id=1, source_target_pairs={{0,18},{1,19},{2,16},{3,17},{16,2},{17,3},{18,0},{19,1},{4,22},{5,... | collective-permute-start | bytes 98312 | tf_op jit(solution)/shard_map/ppermute | solution.py:296
  16.3 0.0 collective-permute-start.7
  16.4 0.0 collective-permute-done.5
  16.4 2.3 %collective-permute-done.6 = bf16[2,4,16,128]{3,2,1,0:T(8,128)(2,1)S(1)} collective-permute-done((bf16[2,4,16,128]{3,2,1,0:T(8,128)(2,1)S(1)}, bf16[2,4,16,128]{3,2,1,0:T(8,128)(2,1)S(1)}, u32[]{:S(2)}, u32[]{:S(2)}) %collective-permute-start.6) | collective-permute-done | bytes 32800 | tf_op jit(solution)/shard_map/ppermute | solution.py:296
  18.7 1.6 %collective-permute-done.7 = bf16[2,4,16,128]{3,2,1,0:T(8,128)(2,1)S(1)} collective-permute-done((bf16[2,4,16,128]{3,2,1,0:T(8,128)(2,1)S(1)}, bf16[2,4,16,128]{3,2,1,0:T(8,128)(2,1)S(1)}, u32[]{:S(2)}, u32[]{:S(2)}) %collective-permute-start.7) | collective-permute-done | bytes 32800 | tf_op jit(solution)/shard_map/ppermute | solution.py:296
  20.3 0.7 %copy.15 = f32[2,2,4,16,128]{4,3,2,1,0:T(8,128)} copy(f32[2,2,4,16,128]{4,3,2,0,1:T(8,128)S(1)} %pad_maximum_fusion) | data formatting | bytes 262144 | tf_op jit(solution)/shard_map/stack | solution.py:304
  (7 shorter events, 0.1 us)
Async XLA Ops:
  0.0 5.2 %copy-start = (bf16[16,128,128]{2,1,0:T(8,128)(2,1)S(1)}, bf16[16,128,128]{2,1,0:T(8,128)(2,1)}, u32[]{:S(2)}) copy-start(bf16[16,128,128]{2,1,0:T(8,128)(2,1)} %param.7) | copy-start | bytes 1572868
  0.9 5.8 %collective-permute-start.1 = (bf16[2,128,128]{2,1,0:T(8,128)(2,1)S(1)}, bf16[2,128,128]{2,1,0:T(8,128)(2,1)S(1)}, u32[]{:S(2)}, u32[]{:S(2)}) collective-permute-start(bf16[2,128,128]{2,1,0:T(8,128)(2,1)S(1)} %broadcast_select_fusion.r_4_), channel_id=1, source_target_pairs={{0,1},{1,0},{2,3},{3,2},{4,5},{5,4},{6,7},{7,6},{8,9},{9,8},{10,11... | collective-permute-start | bytes 196616 | tf_op jit(solution)/shard_map/ppermute | solution.py:262
  1.5 5.3 %collective-permute-start.2 = (bf16[2,128,128]{2,1,0:T(8,128)(2,1)S(1)}, bf16[2,128,128]{2,1,0:T(8,128)(2,1)S(1)}, u32[]{:S(2)}, u32[]{:S(2)}) collective-permute-start(bf16[2,128,128]{2,1,0:T(8,128)(2,1)S(1)} %broadcast_select_fusion.r_4_), channel_id=1, source_target_pairs={{0,2},{1,3},{2,0},{3,1},{4,6},{5,7},{6,4},{7,5},{8,10},{9,11},{10,... | collective-permute-start | bytes 196616 | tf_op jit(solution)/shard_map/ppermute | solution.py:260
  5.0 1.7 %collective-permute-start = (bf16[4,128,128]{2,1,0:T(8,128)(2,1)S(1)}, bf16[4,128,128]{2,1,0:T(8,128)(2,1)S(1)}, u32[]{:S(2)}, u32[]{:S(2)}) collective-permute-start(bf16[4,128,128]{2,1,0:T(8,128)(2,1)S(1)} %get-tuple-element.5), channel_id=1, source_target_pairs={{0,1},{1,0},{2,3},{3,2},{4,5},{5,4},{6,7},{7,6},{8,9},{9,8},{10,11... | collective-permute-start | bytes 393224 | tf_op jit(solution)/shard_map/ppermute | solution.py:263
  6.7 1.6 %collective-permute-start.3 = (bf16[1,2,128,128]{3,2,1,0:T(8,128)(2,1)S(1)}, bf16[1,2,128,128]{3,2,1,0:T(8,128)(2,1)S(1)}, u32[]{:S(2)}, u32[]{:S(2)}) collective-permute-start(bf16[1,2,128,128]{3,2,1,0:T(8,128)(2,1)S(1)} %bitcast.65), channel_id=1, source_target_pairs={{0,1},{1,0},{2,3},{3,2},{4,5},{5,4},{6,7},{7,6},{8,9},{9,8},{10,11... | collective-permute-start | bytes 196616 | tf_op jit(solution)/shard_map/ppermute | solution.py:269
  10.4 1.6 %collective-permute-start.4 = (f32[4,2,2,16,128]{4,3,2,1,0:T(8,128)S(1)}, f32[4,2,2,16,128]{4,3,2,1,0:T(8,128)S(1)}, u32[]{:S(2)}, u32[]{:S(2)}) collective-permute-start(f32[4,2,2,16,128]{4,3,2,1,0:T(8,128)S(1)} %dynamic-slice_bitcast_fusion), channel_id=1, source_target_pairs={{0,1},{1,0},{2,3},{3,2},{4,5},{5,4},{6,7},{7,6},{8,9},{9,8},{10,11... | collective-permute-start | bytes 393224 | tf_op jit(solution)/shard_map/ppermute | solution.py:280
  12.0 4.4 %collective-permute-start.5 = (bf16[2,4,16,128]{3,2,1,0:T(8,128)(2,1)S(1)}, bf16[2,4,16,128]{3,2,1,0:T(8,128)(2,1)S(1)}, u32[]{:S(2)}, u32[]{:S(2)}) collective-permute-start(bf16[2,4,16,128]{3,2,1,0:T(8,128)(2,1)S(1)} %get-tuple-element.12), channel_id=1, source_target_pairs={{0,16},{1,17},{2,18},{3,19},{16,0},{17,1},{18,2},{19,3},{4,20},{5,... | collective-permute-start | bytes 98312 | tf_op jit(solution)/shard_map/ppermute | solution.py:296
  13.8 4.9 %collective-permute-start.6 = (bf16[2,4,16,128]{3,2,1,0:T(8,128)(2,1)S(1)}, bf16[2,4,16,128]{3,2,1,0:T(8,128)(2,1)S(1)}, u32[]{:S(2)}, u32[]{:S(2)}) collective-permute-start(bf16[2,4,16,128]{3,2,1,0:T(8,128)(2,1)S(1)} %get-tuple-element.13), channel_id=1, source_target_pairs={{0,18},{1,19},{2,16},{3,17},{16,2},{17,3},{18,0},{19,1},{4,22},{5,... | collective-permute-start | bytes 98312 | tf_op jit(solution)/shard_map/ppermute | solution.py:296
  16.3 3.9 %collective-permute-start.7 = (bf16[2,4,16,128]{3,2,1,0:T(8,128)(2,1)S(1)}, bf16[2,4,16,128]{3,2,1,0:T(8,128)(2,1)S(1)}, u32[]{:S(2)}, u32[]{:S(2)}) collective-permute-start(bf16[2,4,16,128]{3,2,1,0:T(8,128)(2,1)S(1)} %get-tuple-element.11), channel_id=1, source_target_pairs={{0,2},{1,3},{2,0},{3,1},{16,18},{17,19},{18,16},{19,17},{4,6},{5,7... | collective-permute-start | bytes 98312 | tf_op jit(solution)/shard_map/ppermute | solution.py:296

commit v4 on v3

--- a/solution.py
+++ b/solution.py
@@ -256,7 +256,7 @@
     kv = jnp.where(lax.broadcasted_iota(jnp.int32, (2, tokens, dh), 0) == 0, keys, values)
     hops = []
     for k in range(1, chips):
-        ring = [(i, (i + 2 * k) % count) for i in range(count)]
+        ring = [(i, (i + 2 * k) % count ^ 1) for i in range(count)]
         hops.append(lax.ppermute(kv, "seq", ring))
     place = jnp.stack([core, chip]).astype(jnp.int32)
     kv_pair = lax.ppermute(kv, "seq", swap)
@@ -276,8 +276,12 @@
         hop_pair,
     )
     grad = grad.reshape(hn, groups, chips, 2, lines, feats)
-    keep = lax.dynamic_index_in_dim(grad, core, 3, False)
-    got = lax.ppermute(lax.dynamic_index_in_dim(grad, 1 - core, 3, False), "seq", swap)
+    chip_of = lax.broadcasted_iota(jnp.int32, (1, groups, chips, 1, 1), 2)
+    here = (lax.broadcasted_iota(jnp.int32, chip_of.shape, 1) == grp) & (chip_of == chip)
+    straight = lax.dynamic_index_in_dim(grad, core, 3, False)
+    crossed = lax.dynamic_index_in_dim(grad, 1 - core, 3, False)
+    keep = jnp.where(here, straight, crossed)
+    got = lax.ppermute(jnp.where(here, crossed, straight), "seq", swap)
     low = core == 0
     part = jnp.stack([jnp.where(low, keep, got), jnp.where(low, got, keep)])
 
@@ -288,7 +292,7 @@
     received = [rows_for(0, 0)] + [0.0] * (groups - 1)
     for turn, ahead in sends(groups, chips):
         route = [
-            (g * count + 2 * y + c, (g + turn) % groups * count + 2 * ((y + ahead) % chips) + c)
+            (g * count + 2 * y + c, (g + turn) % groups * count + 2 * ((y + ahead) % chips) + 1 - c)
             for g in range(groups)
             for y in range(chips)
             for c in range(2)

time: 21.1 us -> 20 us (0.948)
  waiting for transfers between devices: 6.26 us -> 5.4 us
  starting transfers between devices: 8.3 us -> 7.88 us
  other arithmetic: 1.07 us -> 1.31 us
    ppermute x3, waiting for transfers between devices: 3.88 us -> 3.33 us  [per_device(): lax.ppermute(rows_for(turn, ahead).astype(WIRE), ('grp', 'seq'), route)]
    ppermute x3, starting transfers between devices: 4.39 us -> 4.01 us  [per_device(): lax.ppermute(rows_for(turn, ahead).astype(WIRE), ('grp', 'seq'), route)]
    ppermute x1, waiting for transfers between devices: 1.38 us -> 1.08 us  [per_device(): hops.append(lax.ppermute(kv, 'seq', ring))]
  transfers between devices with their start and end apart: 8 -> 8, of which waited for: 4 -> 4; matrix products, arithmetic and copies ran while one was open for 5% -> 6% of each run, Pallas kernels for 8% -> 8%
where the time goes in v4:
time: 20 us; the launch traced here: 19.9 us
  starting transfers between devices  7.88 us (39%)
  waiting for transfers between devices  5.4 us (27%)
  Pallas kernels  3.57 us (18%)
  local copies, waits for them, and re-layouts  1.66 us (8%)
  other arithmetic  1.31 us (7%)
    ppermute x3, starting transfers between devices, per_device(): lax.ppermute(rows_for(turn, ahead).astype(WIRE), ('grp', 'seq'), route)  4.01 us
    pallas_call x2, Pallas kernels, call(): pl.pallas_call(function, in_specs=[pl.BlockSpec(memory_space=pltpu.SMEM)]...  3.57 us
    ppermute x3, waiting for transfers between devices, per_device(): lax.ppermute(rows_for(turn, ahead).astype(WIRE), ('grp', 'seq'), route)  3.33 us
    ppermute x1, starting transfers between devices, per_device(): hops.append(lax.ppermute(kv, 'seq', ring))  2.62 us
    ppermute x1, waiting for transfers between devices, per_device(): hops.append(lax.ppermute(kv, 'seq', ring))  1.08 us
    squeeze x2, local copies, waits for them, and re-layouts, mine(): return lax.dynamic_index_in_dim(split_heads, half * groups + grp, 0, False)  0.99 us
    ppermute x1, waiting for transfers between devices, per_device(): got = lax.ppermute(jnp.where(here, crossed, straight), 'seq', swap)  0.99 us
    select_n x1, other arithmetic, per_device(): jnp.where(lax.broadcasted_iota(jnp.int32, (2, tokens, dh), 0) == 0, keys,...  0.91 us
  transfers between devices with their start and end apart: 8, of which 4 were waited for; matrix products, arithmetic and copies ran while one was open for 6% of the time, Pallas kernels for 8%

profile of v4, /device:TPU:0, one launch (start us, length us, event | category | flops | bytes accessed | tf_op | source)
XLA Modules:
  0.0 19.9 jit_solution(10972990652694336452)
XLA Ops:
  0.0 0.9 %broadcast_select_fusion.r_4_ = bf16[2,128,128]{2,1,0:T(8,128)(2,1)S(1)} fusion(pred[2]{0:T(512)(128)(4,1)S(1)} %iota_compare_fusion, bf16[128,128]{1,0:T(8,128)(2,1)} %bitcast.73, bf16[128,128]{1,0:T(8,128)(2,1)} %bitcast.74), kind=kLoop, calls=%fused_computation.30 | loop fusion | flops 32768 | bytes 131074 | tf_op jit(solution)/shard_map/jit(_where)/select_n | solution.py:256
  0.9 0.5 %collective-permute-start.1 = (bf16[2,128,128]{2,1,0:T(8,128)(2,1)S(1)}, bf16[2,128,128]{2,1,0:T(8,128)(2,1)S(1)}, u32[]{:S(2)}, u32[]{:S(2)}) collective-permute-start(bf16[2,128,128]{2,1,0:T(8,128)(2,1)S(1)} %broadcast_select_fusion.r_4_), channel_id=1, source_target_pairs={{0,1},{1,0},{2,3},{3,2},{4,5},{5,4},{6,7},{7,6},{8,9},{9,8},{10,11... | collective-permute-start | bytes 196616 | tf_op jit(solution)/shard_map/ppermute | solution.py:262
  1.5 2.6 %collective-permute-start.2 = (bf16[2,128,128]{2,1,0:T(8,128)(2,1)S(1)}, bf16[2,128,128]{2,1,0:T(8,128)(2,1)S(1)}, u32[]{:S(2)}, u32[]{:S(2)}) collective-permute-start(bf16[2,128,128]{2,1,0:T(8,128)(2,1)S(1)} %broadcast_select_fusion.r_4_), channel_id=1, source_target_pairs={{0,3},{1,2},{2,1},{3,0},{4,7},{5,6},{6,5},{7,4},{8,11},{9,10},{10,... | collective-permute-start | bytes 196616 | tf_op jit(solution)/shard_map/ppermute | solution.py:260
  4.1 1.0 %dynamic-slice_bitcast_fusion.1 = (bf16[4,128,128]{2,1,0:T(8,128)(2,1)S(1)}, bf16[4,128,128]{2,1,0:T(8,128)(2,1)S(1)}) fusion(bf16[4,4,128,128]{3,2,1,0:T(8,128)(2,1)} %bitcast.72, s32[]{:T(128)S(6)} %select_n.115, s32[]{:T(128)S(6)} %select_n.114), kind=kLoop, calls=%fused_computation.14 | loop fusion | bytes 524296 | tf_op jit(solution)/shard_map/jit(dynamic_index_in_dim)/squeeze | solution.py:254
  5.1 0.1 collective-permute-start
  5.2 0.1 broadcast_and_fusion
  5.3 0.1 pad_add_fusion.r_0_
  5.4 1.1 %collective-permute-done.2 = bf16[2,128,128]{2,1,0:T(8,128)(2,1)S(1)} collective-permute-done((bf16[2,128,128]{2,1,0:T(8,128)(2,1)S(1)}, bf16[2,128,128]{2,1,0:T(8,128)(2,1)S(1)}, u32[]{:S(2)}, u32[]{:S(2)}) %collective-permute-start.2) | collective-permute-done | bytes 65568 | tf_op jit(solution)/shard_map/ppermute | solution.py:260
  6.5 0.1 collective-permute-start.3
  6.6 0.0 collective-permute-done.1.r_5_
  6.6 1.6 %shard_map.46.r_6_ = f32[4,264,256]{2,1,0:T(8,128)S(1)} custom-call(s32[2]{0:T(128)S(1)} %pad_add_fusion.r_0_, bf16[4,128,128]{2,1,0:T(8,128)(2,1)S(1)} %get-tuple-element.6.r_1_, bf16[4,128,128]{2,1,0:T(8,128)(2,1)S(1)} %collective-permute-done.r_2_, bf16[4,128,128]{2,1,0:T(8,128)(2,1)S(1)} %dynamic-slice_bitcast_fusion.r_3_, ...), custom_call_target="tpu_custom_call" | custom-call | flops 2000000000 | bytes 10000000 | tf_op jit(solution)/shard_map/pallas_call | solution.py:229
  8.2 0.0 collective-permute-done.3.r_8_
  8.2 2.0 %shard_map.47 = f32[4,128,128]{2,1,0:T(8,128)S(1)} custom-call(s32[2]{0:T(128)S(1)} %pad_add_fusion.r_0_, bf16[4,128,128]{2,1,0:T(8,128)(2,1)S(1)} %get-tuple-element.6.r_1_, bf16[4,128,128]{2,1,0:T(8,128)(2,1)S(1)} %collective-permute-done.r_2_, bf16[4,128,128]{2,1,0:T(8,128)(2,1)S(1)} %dynamic-slice_bitcast_fusion.r_3_, ...), custom_call_target="tpu_custom_call" | custom-call | flops 2000000000 | bytes 10000000 | tf_op jit(solution)/shard_map/pallas_call | solution.py:229
  10.2 0.1 bitcast_select_fusion
  10.3 0.5 %collective-permute-start.4 = (f32[4,2,2,16,128]{4,3,2,1,0:T(8,128)S(1)}, f32[4,2,2,16,128]{4,3,2,1,0:T(8,128)S(1)}, u32[]{:S(2)}, u32[]{:S(2)}) collective-permute-start(f32[4,2,2,16,128]{4,3,2,1,0:T(8,128)S(1)} %bitcast_select_fusion), channel_id=1, source_target_pairs={{0,1},{1,0},{2,3},{3,2},{4,5},{5,4},{6,7},{7,6},{8,9},{9,8},{10,11... | collective-permute-start | bytes 393224 | tf_op jit(solution)/shard_map/ppermute | solution.py:284
  10.7 1.0 %collective-permute-done.4 = f32[4,2,2,16,128]{4,3,2,1,0:T(8,128)S(1)} collective-permute-done((f32[4,2,2,16,128]{4,3,2,1,0:T(8,128)S(1)}, f32[4,2,2,16,128]{4,3,2,1,0:T(8,128)S(1)}, u32[]{:S(2)}, u32[]{:S(2)}) %collective-permute-start.4) | collective-permute-done | bytes 131104 | tf_op jit(solution)/shard_map/ppermute | solution.py:284
  11.7 0.1 select_bitcast_fusion.1
  11.8 1.4 %collective-permute-start.5 = (bf16[2,4,16,128]{3,2,1,0:T(8,128)(2,1)S(1)}, bf16[2,4,16,128]{3,2,1,0:T(8,128)(2,1)S(1)}, u32[]{:S(2)}, u32[]{:S(2)}) collective-permute-start(bf16[2,4,16,128]{3,2,1,0:T(8,128)(2,1)S(1)} %get-tuple-element.12), channel_id=1, source_target_pairs={{0,17},{1,16},{2,19},{3,18},{16,1},{17,0},{18,3},{19,2},{4,21},{5,... | collective-permute-start | bytes 98312 | tf_op jit(solution)/shard_map/ppermute | solution.py:300
  13.3 2.5 %collective-permute-start.6 = (bf16[2,4,16,128]{3,2,1,0:T(8,128)(2,1)S(1)}, bf16[2,4,16,128]{3,2,1,0:T(8,128)(2,1)S(1)}, u32[]{:S(2)}, u32[]{:S(2)}) collective-permute-start(bf16[2,4,16,128]{3,2,1,0:T(8,128)(2,1)S(1)} %get-tuple-element.13), channel_id=1, source_target_pairs={{0,19},{1,18},{2,17},{3,16},{16,3},{17,2},{18,1},{19,0},{4,23},{5,... | collective-permute-start | bytes 98312 | tf_op jit(solution)/shard_map/ppermute | solution.py:300
  15.8 0.0 collective-permute-start.7
  15.8 0.0 collective-permute-done.5
  15.8 2.3 %collective-permute-done.6 = bf16[2,4,16,128]{3,2,1,0:T(8,128)(2,1)S(1)} collective-permute-done((bf16[2,4,16,128]{3,2,1,0:T(8,128)(2,1)S(1)}, bf16[2,4,16,128]{3,2,1,0:T(8,128)(2,1)S(1)}, u32[]{:S(2)}, u32[]{:S(2)}) %collective-permute-start.6) | collective-permute-done | bytes 32800 | tf_op jit(solution)/shard_map/ppermute | solution.py:300
  18.1 1.0 %collective-permute-done.7 = bf16[2,4,16,128]{3,2,1,0:T(8,128)(2,1)S(1)} collective-permute-done((bf16[2,4,16,128]{3,2,1,0:T(8,128)(2,1)S(1)}, bf16[2,4,16,128]{3,2,1,0:T(8,128)(2,1)S(1)}, u32[]{:S(2)}, u32[]{:S(2)}) %collective-permute-start.7) | collective-permute-done | bytes 32800 | tf_op jit(solution)/shard_map/ppermute | solution.py:300
  19.2 0.7 %copy.15 = f32[2,2,4,16,128]{4,3,2,1,0:T(8,128)} copy(f32[2,2,4,16,128]{4,3,2,0,1:T(8,128)S(1)} %pad_maximum_fusion) | data formatting | bytes 262144 | tf_op jit(solution)/shard_map/stack | solution.py:308
  (9 shorter events, 0.1 us)
Async XLA Ops:
  0.0 5.3 %copy-start = (bf16[16,128,128]{2,1,0:T(8,128)(2,1)S(1)}, bf16[16,128,128]{2,1,0:T(8,128)(2,1)}, u32[]{:S(2)}) copy-start(bf16[16,128,128]{2,1,0:T(8,128)(2,1)} %param.7) | copy-start | bytes 1572868
  0.9 5.7 %collective-permute-start.1 = (bf16[2,128,128]{2,1,0:T(8,128)(2,1)S(1)}, bf16[2,128,128]{2,1,0:T(8,128)(2,1)S(1)}, u32[]{:S(2)}, u32[]{:S(2)}) collective-permute-start(bf16[2,128,128]{2,1,0:T(8,128)(2,1)S(1)} %broadcast_select_fusion.r_4_), channel_id=1, source_target_pairs={{0,1},{1,0},{2,3},{3,2},{4,5},{5,4},{6,7},{7,6},{8,9},{9,8},{10,11... | collective-permute-start | bytes 196616 | tf_op jit(solution)/shard_map/ppermute | solution.py:262
  1.5 5.0 %collective-permute-start.2 = (bf16[2,128,128]{2,1,0:T(8,128)(2,1)S(1)}, bf16[2,128,128]{2,1,0:T(8,128)(2,1)S(1)}, u32[]{:S(2)}, u32[]{:S(2)}) collective-permute-start(bf16[2,128,128]{2,1,0:T(8,128)(2,1)S(1)} %broadcast_select_fusion.r_4_), channel_id=1, source_target_pairs={{0,3},{1,2},{2,1},{3,0},{4,7},{5,6},{6,5},{7,4},{8,11},{9,10},{10,... | collective-permute-start | bytes 196616 | tf_op jit(solution)/shard_map/ppermute | solution.py:260
  5.1 1.5 %collective-permute-start = (bf16[4,128,128]{2,1,0:T(8,128)(2,1)S(1)}, bf16[4,128,128]{2,1,0:T(8,128)(2,1)S(1)}, u32[]{:S(2)}, u32[]{:S(2)}) collective-permute-start(bf16[4,128,128]{2,1,0:T(8,128)(2,1)S(1)} %get-tuple-element.5), channel_id=1, source_target_pairs={{0,1},{1,0},{2,3},{3,2},{4,5},{5,4},{6,7},{7,6},{8,9},{9,8},{10,11... | collective-permute-start | bytes 393224 | tf_op jit(solution)/shard_map/ppermute | solution.py:263
  6.5 1.7 %collective-permute-start.3 = (bf16[1,2,128,128]{3,2,1,0:T(8,128)(2,1)S(1)}, bf16[1,2,128,128]{3,2,1,0:T(8,128)(2,1)S(1)}, u32[]{:S(2)}, u32[]{:S(2)}) collective-permute-start(bf16[1,2,128,128]{3,2,1,0:T(8,128)(2,1)S(1)} %bitcast.70), channel_id=1, source_target_pairs={{0,1},{1,0},{2,3},{3,2},{4,5},{5,4},{6,7},{7,6},{8,9},{9,8},{10,11... | collective-permute-start | bytes 196616 | tf_op jit(solution)/shard_map/ppermute | solution.py:269
  10.3 1.4 %collective-permute-start.4 = (f32[4,2,2,16,128]{4,3,2,1,0:T(8,128)S(1)}, f32[4,2,2,16,128]{4,3,2,1,0:T(8,128)S(1)}, u32[]{:S(2)}, u32[]{:S(2)}) collective-permute-start(f32[4,2,2,16,128]{4,3,2,1,0:T(8,128)S(1)} %bitcast_select_fusion), channel_id=1, source_target_pairs={{0,1},{1,0},{2,3},{3,2},{4,5},{5,4},{6,7},{7,6},{8,9},{9,8},{10,11... | collective-permute-start | bytes 393224 | tf_op jit(solution)/shard_map/ppermute | solution.py:284
  11.8 4.0 %collective-permute-start.5 = (bf16[2,4,16,128]{3,2,1,0:T(8,128)(2,1)S(1)}, bf16[2,4,16,128]{3,2,1,0:T(8,128)(2,1)S(1)}, u32[]{:S(2)}, u32[]{:S(2)}) collective-permute-start(bf16[2,4,16,128]{3,2,1,0:T(8,128)(2,1)S(1)} %get-tuple-element.12), channel_id=1, source_target_pairs={{0,17},{1,16},{2,19},{3,18},{16,1},{17,0},{18,3},{19,2},{4,21},{5,... | collective-permute-start | bytes 98312 | tf_op jit(solution)/shard_map/ppermute | solution.py:300
  13.3 4.8 %collective-permute-start.6 = (bf16[2,4,16,128]{3,2,1,0:T(8,128)(2,1)S(1)}, bf16[2,4,16,128]{3,2,1,0:T(8,128)(2,1)S(1)}, u32[]{:S(2)}, u32[]{:S(2)}) collective-permute-start(bf16[2,4,16,128]{3,2,1,0:T(8,128)(2,1)S(1)} %get-tuple-element.13), channel_id=1, source_target_pairs={{0,19},{1,18},{2,17},{3,16},{16,3},{17,2},{18,1},{19,0},{4,23},{5,... | collective-permute-start | bytes 98312 | tf_op jit(solution)/shard_map/ppermute | solution.py:300
  15.8 3.4 %collective-permute-start.7 = (bf16[2,4,16,128]{3,2,1,0:T(8,128)(2,1)S(1)}, bf16[2,4,16,128]{3,2,1,0:T(8,128)(2,1)S(1)}, u32[]{:S(2)}, u32[]{:S(2)}) collective-permute-start(bf16[2,4,16,128]{3,2,1,0:T(8,128)(2,1)S(1)} %get-tuple-element.11), channel_id=1, source_target_pairs={{0,3},{1,2},{2,1},{3,0},{16,19},{17,18},{18,17},{19,16},{4,7},{5,6... | collective-permute-start | bytes 98312 | tf_op jit(solution)/shard_map/ppermute | solution.py:300

commit v5 on v4

--- a/solution.py
+++ b/solution.py
@@ -281,7 +281,8 @@
     straight = lax.dynamic_index_in_dim(grad, core, 3, False)
     crossed = lax.dynamic_index_in_dim(grad, 1 - core, 3, False)
     keep = jnp.where(here, straight, crossed)
-    got = lax.ppermute(jnp.where(here, crossed, straight), "seq", swap)
+    got = lax.ppermute(jnp.where(here, crossed, straight).astype(WIRE), "seq", swap)
+    got = got.astype(F32)
     low = core == 0
     part = jnp.stack([jnp.where(low, keep, got), jnp.where(low, got, keep)])
 
@@ -311,7 +312,7 @@
 def sends(groups, chips):
     across = [(turn, ahead) for ahead in range(1, chips) for turn in reversed(range(groups))]
     beside = [(turn, 0) for turn in range(1, groups)]
-    return beside + across
+    return across[:1] + beside + across[1:]
 
 
 def solution(mesh):

time: 20 us -> 19.9 us (level)
  transfers between devices with their start and end apart: 8 -> 8, of which waited for: 4 -> 5; matrix products, arithmetic and copies ran while one was open for 6% -> 6% of each run, Pallas kernels for 8% -> 8%
where the time goes in v5:
time: 19.9 us; the launch traced here: 19.7 us
  starting transfers between devices  7.92 us (40%)
  waiting for transfers between devices  5.23 us (26%)
  Pallas kernels  3.57 us (18%)
  local copies, waits for them, and re-layouts  1.66 us (8%)
  other arithmetic  1.3 us (7%)
    ppermute x3, starting transfers between devices, per_device(): lax.ppermute(rows_for(turn, ahead).astype(WIRE), ('grp', 'seq'), route)  4.08 us
    pallas_call x2, Pallas kernels, call(): pl.pallas_call(function, in_specs=[pl.BlockSpec(memory_space=pltpu.SMEM)]...  3.57 us
    ppermute x3, waiting for transfers between devices, per_device(): lax.ppermute(rows_for(turn, ahead).astype(WIRE), ('grp', 'seq'), route)  3.24 us
    ppermute x1, starting transfers between devices, per_device(): hops.append(lax.ppermute(kv, 'seq', ring))  2.62 us
    ppermute x1, waiting for transfers between devices, per_device(): hops.append(lax.ppermute(kv, 'seq', ring))  1.08 us
    squeeze x2, local copies, waits for them, and re-layouts, mine(): return lax.dynamic_index_in_dim(split_heads, half * groups + grp, 0, False)  0.99 us
    select_n x1, other arithmetic, per_device(): jnp.where(lax.broadcasted_iota(jnp.int32, (2, tokens, dh), 0) == 0, keys,...  0.91 us
    ppermute x1, waiting for transfers between devices, per_device(): lax.ppermute(jnp.where(here, crossed, straight).astype(WIRE), 'seq', swap)  0.9 us
  transfers between devices with their start and end apart: 8, of which 5 were waited for; matrix products, arithmetic and copies ran while one was open for 6% of the time, Pallas kernels for 8%

profile of v5, /device:TPU:0, one launch (start us, length us, event | category | flops | bytes accessed | tf_op | source)
XLA Modules:
  0.0 19.7 jit_solution(13359969727475941891)
XLA Ops:
  0.0 0.9 %broadcast_select_fusion.r_4_ = bf16[2,128,128]{2,1,0:T(8,128)(2,1)S(1)} fusion(pred[2]{0:T(512)(128)(4,1)S(1)} %iota_compare_fusion, bf16[128,128]{1,0:T(8,128)(2,1)} %bitcast.75, bf16[128,128]{1,0:T(8,128)(2,1)} %bitcast.76), kind=kLoop, calls=%fused_computation.33 | loop fusion | flops 32768 | bytes 131074 | tf_op jit(solution)/shard_map/jit(_where)/select_n | solution.py:256
  0.9 0.5 %collective-permute-start.1 = (bf16[2,128,128]{2,1,0:T(8,128)(2,1)S(1)}, bf16[2,128,128]{2,1,0:T(8,128)(2,1)S(1)}, u32[]{:S(2)}, u32[]{:S(2)}) collective-permute-start(bf16[2,128,128]{2,1,0:T(8,128)(2,1)S(1)} %broadcast_select_fusion.r_4_), channel_id=1, source_target_pairs={{0,1},{1,0},{2,3},{3,2},{4,5},{5,4},{6,7},{7,6},{8,9},{9,8},{10,11... | collective-permute-start | bytes 196616 | tf_op jit(solution)/shard_map/ppermute | solution.py:262
  1.5 2.6 %collective-permute-start.2 = (bf16[2,128,128]{2,1,0:T(8,128)(2,1)S(1)}, bf16[2,128,128]{2,1,0:T(8,128)(2,1)S(1)}, u32[]{:S(2)}, u32[]{:S(2)}) collective-permute-start(bf16[2,128,128]{2,1,0:T(8,128)(2,1)S(1)} %broadcast_select_fusion.r_4_), channel_id=1, source_target_pairs={{0,3},{1,2},{2,1},{3,0},{4,7},{5,6},{6,5},{7,4},{8,11},{9,10},{10,... | collective-permute-start | bytes 196616 | tf_op jit(solution)/shard_map/ppermute | solution.py:260
  4.1 1.0 %dynamic-slice_bitcast_fusion.1 = (bf16[4,128,128]{2,1,0:T(8,128)(2,1)S(1)}, bf16[4,128,128]{2,1,0:T(8,128)(2,1)S(1)}) fusion(bf16[4,4,128,128]{3,2,1,0:T(8,128)(2,1)} %bitcast.74, s32[]{:T(128)S(6)} %select_n.115, s32[]{:T(128)S(6)} %select_n.114), kind=kLoop, calls=%fused_computation.17 | loop fusion | bytes 524296 | tf_op jit(solution)/shard_map/jit(dynamic_index_in_dim)/squeeze | solution.py:254
  5.1 0.1 collective-permute-start
  5.2 0.1 broadcast_and_fusion
  5.3 0.1 pad_add_fusion.r_0_
  5.4 1.1 %collective-permute-done.2 = bf16[2,128,128]{2,1,0:T(8,128)(2,1)S(1)} collective-permute-done((bf16[2,128,128]{2,1,0:T(8,128)(2,1)S(1)}, bf16[2,128,128]{2,1,0:T(8,128)(2,1)S(1)}, u32[]{:S(2)}, u32[]{:S(2)}) %collective-permute-start.2) | collective-permute-done | bytes 65568 | tf_op jit(solution)/shard_map/ppermute | solution.py:260
  6.5 0.1 collective-permute-start.3
  6.6 0.0 collective-permute-done.1.r_5_
  6.6 1.6 %shard_map.46.r_6_ = f32[4,264,256]{2,1,0:T(8,128)S(1)} custom-call(s32[2]{0:T(128)S(1)} %pad_add_fusion.r_0_, bf16[4,128,128]{2,1,0:T(8,128)(2,1)S(1)} %get-tuple-element.6.r_1_, bf16[4,128,128]{2,1,0:T(8,128)(2,1)S(1)} %collective-permute-done.r_2_, bf16[4,128,128]{2,1,0:T(8,128)(2,1)S(1)} %dynamic-slice_bitcast_fusion.r_3_, ...), custom_call_target="tpu_custom_call" | custom-call | flops 2000000000 | bytes 10000000 | tf_op jit(solution)/shard_map/pallas_call | solution.py:229
  8.2 0.0 collective-permute-done.3.r_8_
  8.2 2.0 %shard_map.47 = f32[4,128,128]{2,1,0:T(8,128)S(1)} custom-call(s32[2]{0:T(128)S(1)} %pad_add_fusion.r_0_, bf16[4,128,128]{2,1,0:T(8,128)(2,1)S(1)} %get-tuple-element.6.r_1_, bf16[4,128,128]{2,1,0:T(8,128)(2,1)S(1)} %collective-permute-done.r_2_, bf16[4,128,128]{2,1,0:T(8,128)(2,1)S(1)} %dynamic-slice_bitcast_fusion.r_3_, ...), custom_call_target="tpu_custom_call" | custom-call | flops 2000000000 | bytes 10000000 | tf_op jit(solution)/shard_map/pallas_call | solution.py:229
  10.2 0.1 fusion.2
  10.3 0.4 %collective-permute-start.4 = (bf16[4,2,2,16,128]{4,3,2,1,0:T(8,128)(2,1)S(1)}, bf16[4,2,2,16,128]{4,3,2,1,0:T(8,128)(2,1)S(1)}, u32[]{:S(2)}, u32[]{:S(2)}) collective-permute-start(bf16[4,2,2,16,128]{4,3,2,1,0:T(8,128)(2,1)S(1)} %fusion.2), channel_id=1, source_target_pairs={{0,1},{1,0},{2,3},{3,2},{4,5},{5,4},{6,7},{7,6},{8,9},{9,8},{10,11... | collective-permute-start | bytes 196616 | tf_op jit(solution)/shard_map/ppermute | solution.py:284
  10.7 0.9 %collective-permute-done.4 = bf16[4,2,2,16,128]{4,3,2,1,0:T(8,128)(2,1)S(1)} collective-permute-done((bf16[4,2,2,16,128]{4,3,2,1,0:T(8,128)(2,1)S(1)}, bf16[4,2,2,16,128]{4,3,2,1,0:T(8,128)(2,1)S(1)}, u32[]{:S(2)}, u32[]{:S(2)}) %collective-permute-start.4) | collective-permute-done | bytes 65568 | tf_op jit(solution)/shard_map/ppermute | solution.py:284
  11.6 0.1 fusion
  11.7 3.5 %collective-permute-start.5 = (bf16[2,4,16,128]{3,2,1,0:T(8,128)(2,1)S(1)}, bf16[2,4,16,128]{3,2,1,0:T(8,128)(2,1)S(1)}, u32[]{:S(2)}, u32[]{:S(2)}) collective-permute-start(bf16[2,4,16,128]{3,2,1,0:T(8,128)(2,1)S(1)} %get-tuple-element.13), channel_id=1, source_target_pairs={{0,19},{1,18},{2,17},{3,16},{16,3},{17,2},{18,1},{19,0},{4,23},{5,... | collective-permute-start | bytes 98312 | tf_op jit(solution)/shard_map/ppermute | solution.py:301
  15.2 0.5 %collective-permute-start.6 = (bf16[2,4,16,128]{3,2,1,0:T(8,128)(2,1)S(1)}, bf16[2,4,16,128]{3,2,1,0:T(8,128)(2,1)S(1)}, u32[]{:S(2)}, u32[]{:S(2)}) collective-permute-start(bf16[2,4,16,128]{3,2,1,0:T(8,128)(2,1)S(1)} %get-tuple-element.12), channel_id=1, source_target_pairs={{0,17},{1,16},{2,19},{3,18},{16,1},{17,0},{18,3},{19,2},{4,21},{5,... | collective-permute-start | bytes 98312 | tf_op jit(solution)/shard_map/ppermute | solution.py:301
  15.7 0.1 collective-permute-start.7
  15.8 1.2 %collective-permute-done.5 = bf16[2,4,16,128]{3,2,1,0:T(8,128)(2,1)S(1)} collective-permute-done((bf16[2,4,16,128]{3,2,1,0:T(8,128)(2,1)S(1)}, bf16[2,4,16,128]{3,2,1,0:T(8,128)(2,1)S(1)}, u32[]{:S(2)}, u32[]{:S(2)}) %collective-permute-start.5) | collective-permute-done | bytes 32800 | tf_op jit(solution)/shard_map/ppermute | solution.py:301
  17.0 1.6 %collective-permute-done.6 = bf16[2,4,16,128]{3,2,1,0:T(8,128)(2,1)S(1)} collective-permute-done((bf16[2,4,16,128]{3,2,1,0:T(8,128)(2,1)S(1)}, bf16[2,4,16,128]{3,2,1,0:T(8,128)(2,1)S(1)}, u32[]{:S(2)}, u32[]{:S(2)}) %collective-permute-start.6) | collective-permute-done | bytes 32800 | tf_op jit(solution)/shard_map/ppermute | solution.py:301
  18.5 0.5 %collective-permute-done.7 = bf16[2,4,16,128]{3,2,1,0:T(8,128)(2,1)S(1)} collective-permute-done((bf16[2,4,16,128]{3,2,1,0:T(8,128)(2,1)S(1)}, bf16[2,4,16,128]{3,2,1,0:T(8,128)(2,1)S(1)}, u32[]{:S(2)}, u32[]{:S(2)}) %collective-permute-start.7) | collective-permute-done | bytes 32800 | tf_op jit(solution)/shard_map/ppermute | solution.py:301
  19.1 0.7 %copy.15 = f32[2,2,4,16,128]{4,3,2,1,0:T(8,128)} copy(f32[2,2,4,16,128]{4,3,2,0,1:T(8,128)S(1)} %pad_maximum_fusion) | data formatting | bytes 262144 | tf_op jit(solution)/shard_map/stack | solution.py:309
  (9 shorter events, 0.1 us)
Async XLA Ops:
  0.0 5.3 %copy-start = (bf16[16,128,128]{2,1,0:T(8,128)(2,1)S(1)}, bf16[16,128,128]{2,1,0:T(8,128)(2,1)}, u32[]{:S(2)}) copy-start(bf16[16,128,128]{2,1,0:T(8,128)(2,1)} %param.7) | copy-start | bytes 1572868
  0.9 5.7 %collective-permute-start.1 = (bf16[2,128,128]{2,1,0:T(8,128)(2,1)S(1)}, bf16[2,128,128]{2,1,0:T(8,128)(2,1)S(1)}, u32[]{:S(2)}, u32[]{:S(2)}) collective-permute-start(bf16[2,128,128]{2,1,0:T(8,128)(2,1)S(1)} %broadcast_select_fusion.r_4_), channel_id=1, source_target_pairs={{0,1},{1,0},{2,3},{3,2},{4,5},{5,4},{6,7},{7,6},{8,9},{9,8},{10,11... | collective-permute-start | bytes 196616 | tf_op jit(solution)/shard_map/ppermute | solution.py:262
  1.5 5.0 %collective-permute-start.2 = (bf16[2,128,128]{2,1,0:T(8,128)(2,1)S(1)}, bf16[2,128,128]{2,1,0:T(8,128)(2,1)S(1)}, u32[]{:S(2)}, u32[]{:S(2)}) collective-permute-start(bf16[2,128,128]{2,1,0:T(8,128)(2,1)S(1)} %broadcast_select_fusion.r_4_), channel_id=1, source_target_pairs={{0,3},{1,2},{2,1},{3,0},{4,7},{5,6},{6,5},{7,4},{8,11},{9,10},{10,... | collective-permute-start | bytes 196616 | tf_op jit(solution)/shard_map/ppermute | solution.py:260
  5.1 1.5 %collective-permute-start = (bf16[4,128,128]{2,1,0:T(8,128)(2,1)S(1)}, bf16[4,128,128]{2,1,0:T(8,128)(2,1)S(1)}, u32[]{:S(2)}, u32[]{:S(2)}) collective-permute-start(bf16[4,128,128]{2,1,0:T(8,128)(2,1)S(1)} %get-tuple-element.5), channel_id=1, source_target_pairs={{0,1},{1,0},{2,3},{3,2},{4,5},{5,4},{6,7},{7,6},{8,9},{9,8},{10,11... | collective-permute-start | bytes 393224 | tf_op jit(solution)/shard_map/ppermute | solution.py:263
  6.5 1.7 %collective-permute-start.3 = (bf16[1,2,128,128]{3,2,1,0:T(8,128)(2,1)S(1)}, bf16[1,2,128,128]{3,2,1,0:T(8,128)(2,1)S(1)}, u32[]{:S(2)}, u32[]{:S(2)}) collective-permute-start(bf16[1,2,128,128]{3,2,1,0:T(8,128)(2,1)S(1)} %bitcast.72), channel_id=1, source_target_pairs={{0,1},{1,0},{2,3},{3,2},{4,5},{5,4},{6,7},{7,6},{8,9},{9,8},{10,11... | collective-permute-start | bytes 196616 | tf_op jit(solution)/shard_map/ppermute | solution.py:269
  10.3 1.3 %collective-permute-start.4 = (bf16[4,2,2,16,128]{4,3,2,1,0:T(8,128)(2,1)S(1)}, bf16[4,2,2,16,128]{4,3,2,1,0:T(8,128)(2,1)S(1)}, u32[]{:S(2)}, u32[]{:S(2)}) collective-permute-start(bf16[4,2,2,16,128]{4,3,2,1,0:T(8,128)(2,1)S(1)} %fusion.2), channel_id=1, source_target_pairs={{0,1},{1,0},{2,3},{3,2},{4,5},{5,4},{6,7},{7,6},{8,9},{9,8},{10,11... | collective-permute-start | bytes 196616 | tf_op jit(solution)/shard_map/ppermute | solution.py:284
  11.7 5.3 %collective-permute-start.5 = (bf16[2,4,16,128]{3,2,1,0:T(8,128)(2,1)S(1)}, bf16[2,4,16,128]{3,2,1,0:T(8,128)(2,1)S(1)}, u32[]{:S(2)}, u32[]{:S(2)}) collective-permute-start(bf16[2,4,16,128]{3,2,1,0:T(8,128)(2,1)S(1)} %get-tuple-element.13), channel_id=1, source_target_pairs={{0,19},{1,18},{2,17},{3,16},{16,3},{17,2},{18,1},{19,0},{4,23},{5,... | collective-permute-start | bytes 98312 | tf_op jit(solution)/shard_map/ppermute | solution.py:301
  15.2 3.3 %collective-permute-start.6 = (bf16[2,4,16,128]{3,2,1,0:T(8,128)(2,1)S(1)}, bf16[2,4,16,128]{3,2,1,0:T(8,128)(2,1)S(1)}, u32[]{:S(2)}, u32[]{:S(2)}) collective-permute-start(bf16[2,4,16,128]{3,2,1,0:T(8,128)(2,1)S(1)} %get-tuple-element.12), channel_id=1, source_target_pairs={{0,17},{1,16},{2,19},{3,18},{16,1},{17,0},{18,3},{19,2},{4,21},{5,... | collective-permute-start | bytes 98312 | tf_op jit(solution)/shard_map/ppermute | solution.py:301
  15.7 3.4 %collective-permute-start.7 = (bf16[2,4,16,128]{3,2,1,0:T(8,128)(2,1)S(1)}, bf16[2,4,16,128]{3,2,1,0:T(8,128)(2,1)S(1)}, u32[]{:S(2)}, u32[]{:S(2)}) collective-permute-start(bf16[2,4,16,128]{3,2,1,0:T(8,128)(2,1)S(1)} %get-tuple-element.11), channel_id=1, source_target_pairs={{0,3},{1,2},{2,1},{3,0},{16,19},{17,18},{18,17},{19,16},{4,7},{5,6... | collective-permute-start | bytes 98312 | tf_op jit(solution)/shard_map/ppermute | solution.py:301
